TPU v7x, 128 devices: a whole 4x4x4 slice. The times are simulated.
128 devices in a mesh: seq: 32 (over y, x, core), mp: 4 (over z).
Axes of the slice: x: 4, y: 4, z: 4, core: 2. Of those that a mesh axis runs over, the one named last changes fastest.
Arguments:
- y_first: bfloat16 [8192, 4096], P('seq', 'mp'), may hold values from -6 to 6
- x_second: bfloat16 [8192, 4096], P('seq', 'mp'), may hold values from -6 to 6
- grad_first: bfloat16 [8192, 4096], P('seq', 'mp'), may hold values from -6 to 6
- grad_second: bfloat16 [8192, 4096], P('seq', 'mp'), may hold values from -6 to 6
- doc_ids: int32 [8192], P('seq'), may hold values from 0 to 7, never falling along the last dimension, each value on 1 to 4096 neighbouring positions
- norm_gain: float32 [4096], replicated, may hold values from 0.25 to 1.75
- w_query: bfloat16 [4096, 2048], P(None, 'mp'), may hold values from -2 to 2
- w_key: bfloat16 [4096, 512], P(None, 'mp'), may hold values from -2 to 2
- w_value: bfloat16 [4096, 512], P(None, 'mp'), may hold values from -0.09375 to 0.09375
- w_out: bfloat16 [2048, 4096], P('mp'), may hold values from -0.25 to 0.25
Outputs:
- x_first: float32 [8192, 4096], P('seq', 'mp')
- x_grad: float32 [8192, 4096], P('seq', 'mp')
Inputs may be any that keep to these rules, and one draw needn't show every extreme that they name: `doc_ids`: document numbers never fall along the sequence; every document has 1 to 4096 tokens, and one has exactly 4096.
All inputs are finite; a program needn't handle non-finite values.
Results may differ from a plain program's by a relative error of at most 0.0092.
Values may be sent and summed in bfloat16 or wider, within the bound.
A program may use at most 128 MiB of HBM per device.

v0:
```python
import jax
import jax.numpy as jnp
from jax import lax
from jax.sharding import PartitionSpec as P

HEAD_DIM = 128


EPSILON = 1e-05
NEGATIVE = -1e30


def side_by_side(arrays, axis, dim, along):
    both = jnp.concatenate(arrays, axis=along)
    whole, at, done = (lax.all_gather(both, axis, axis=dim, tiled=True), 0, [])
    for a in arrays:
        done.append(lax.slice_in_dim(whole, at, at + a.shape[along], axis=along))
        at += a.shape[along]
    return tuple(done)


def in_order(tiles, dim):
    shape = list(tiles.shape[1:])
    shape[dim] *= tiles.shape[0]
    return jnp.moveaxis(tiles, 0, dim).reshape(shape)


def from_everyone(value, axis):
    copies = jnp.broadcast_to(value, (lax.axis_size(axis), *value.shape))
    return lax.all_to_all(copies, axis, split_axis=0, concat_axis=0, tiled=True)


def gather_directly(value, axis, dim):
    return in_order(from_everyone(value, axis), dim)


def cut_along(value, dim, size):
    shape = value.shape
    tiles = value.reshape(*shape[:dim], size, shape[dim] // size, *shape[dim + 1 :])
    return jnp.moveaxis(tiles, dim, 0)


def sum_at_owner(value, axis, dim):
    size = lax.axis_size(axis)
    tiles = lax.all_to_all(cut_along(value, dim, size), axis, 0, 0, tiled=True)
    return jnp.sum(tiles, axis=0)


def side_by_side_2(arrays, axis, dim, along):
    both = jnp.concatenate(arrays, axis=along)
    whole, at, done = (lax.psum_scatter(both, axis, scatter_dimension=dim, tiled=True), 0, [])
    for a in arrays:
        done.append(lax.slice_in_dim(whole, at, at + a.shape[along], axis=along))
        at += a.shape[along]
    return tuple(done)


def taken_together(value, axis):
    return from_everyone(value, axis).sum(axis=0)


def key_meta(context, row_count, first_key):
    queries, query_pos, query_doc, all_docs, score_scale = context
    key_pos = first_key + jnp.arange(row_count, dtype=jnp.int32)
    key_doc = lax.dynamic_slice_in_dim(all_docs, first_key, row_count, 0)
    allowed = (key_pos[None, :] <= query_pos[:, None]) & (key_doc[None, :] == query_doc[:, None])
    needed = (first_key <= query_pos[-1]) & (key_doc[-1] >= query_doc[0])
    return (allowed[:, None, None, :], needed)


def score_block(context, key_block):
    queries, query_pos, query_doc, all_docs, score_scale = context
    scores = jnp.einsum("qkgd,tkd->qkgt", queries, key_block, preferred_element_type=jnp.float32)
    return scores * score_scale


def forward_step(running, key_flat, value_flat, first_key, context):
    row_count = key_flat.shape[0]
    key_block = key_flat.reshape(row_count, -1, HEAD_DIM)
    value_block = value_flat.reshape(row_count, -1, HEAD_DIM)
    allowed, needed = key_meta(context, row_count, first_key)

    def forward_compute(current):
        row_max, row_total, accum = current
        scores = score_block(context, key_block)
        new_max = jnp.maximum(row_max, jnp.max(jnp.where(allowed, scores, NEGATIVE), axis=-1))
        weights = jnp.where(allowed, jnp.exp(scores - new_max[..., None]), 0.0)
        factor = jnp.exp(row_max - new_max)
        row_total = row_total * factor + jnp.sum(weights, axis=-1)
        accum = accum * factor[..., None] + jnp.einsum(
            "qkgt,tkd->qkgd",
            weights,
            value_block.astype(jnp.float32),
            precision=lax.Precision.HIGHEST,
            preferred_element_type=jnp.float32,
        )
        return (new_max, row_total, accum)

    return lax.cond(needed, forward_compute, lambda current: current, running)


def backward_step(gradients, key_flat, value_flat, first_key, context, back_context):
    queries, query_pos, query_doc, all_docs, score_scale = context
    grad_out, log_totals, deltas = back_context
    row_count = key_flat.shape[0]
    key_block = key_flat.reshape(row_count, -1, HEAD_DIM)
    value_block = value_flat.reshape(row_count, -1, HEAD_DIM)
    allowed, needed = key_meta(context, row_count, first_key)

    def backward_compute(current):
        query_grad, key_grad, value_grad = current
        scores = score_block(context, key_block)
        probs = jnp.where(allowed, jnp.exp(scores - log_totals[..., None]), 0.0)
        prob_grad = jnp.einsum(
            "qkgd,tkd->qkgt", grad_out, value_block, preferred_element_type=jnp.float32
        )
        score_grad = (probs * (prob_grad - deltas[..., None])).astype(jnp.bfloat16)
        query_grad = query_grad + score_scale * jnp.einsum(
            "qkgt,tkd->qkgd", score_grad, key_block, preferred_element_type=jnp.float32
        )
        key_terms = score_scale * jnp.einsum(
            "qkgt,qkgd->tkd", score_grad, queries, preferred_element_type=jnp.float32
        )
        value_terms = jnp.einsum(
            "qkgt,qkgd->tkd",
            probs.astype(jnp.bfloat16),
            grad_out,
            preferred_element_type=jnp.float32,
        )
        key_grad = key_grad + key_terms.reshape(row_count, -1)
        value_grad = value_grad + value_terms.reshape(row_count, -1)
        return (query_grad, key_grad, value_grad)

    return lax.cond(needed, backward_compute, lambda current: current, gradients)


def per_device(
    y_first, x_second, grad_first, grad_second, doc_ids, norm_gain, w_query, w_key, w_value, w_out
):
    tok_rows = y_first.shape[0]
    cycle_size = lax.axis_size("seq")
    cycle_rank = lax.axis_index("seq")
    full_rows, grad_rows = side_by_side((x_second, grad_first), "mp", 1, 0)
    all_docs = gather_directly(doc_ids, "seq", 0)
    inputs = full_rows.astype(jnp.float32)
    inverse_rms = lax.rsqrt(jnp.mean(inputs * inputs, axis=-1, keepdims=True) + EPSILON)
    unit_rows = inputs * inverse_rms
    normed = (unit_rows * norm_gain).astype(jnp.bfloat16)
    kv_local = w_key.shape[1] // HEAD_DIM
    group_size = w_query.shape[1] // HEAD_DIM // kv_local
    queries = jnp.dot(normed, w_query, preferred_element_type=jnp.float32).astype(jnp.bfloat16)
    queries = queries.reshape(tok_rows, kv_local, group_size, HEAD_DIM)
    key_flat = jnp.dot(normed, w_key, preferred_element_type=jnp.float32).astype(jnp.bfloat16)
    value_flat = jnp.dot(normed, w_value, preferred_element_type=jnp.float32).astype(jnp.bfloat16)
    query_pos = cycle_rank * tok_rows + jnp.arange(tok_rows, dtype=jnp.int32)
    context = (queries, query_pos, doc_ids, all_docs, HEAD_DIM ** (-0.5))
    head_shape = (tok_rows, kv_local, group_size)
    start_state = (
        jnp.full(head_shape, NEGATIVE, jnp.float32),
        jnp.zeros(head_shape, jnp.float32),
        jnp.zeros(head_shape + (HEAD_DIM,), jnp.float32),
    )
    every_key, every_value = side_by_side((key_flat, value_flat), "seq", 0, 1)

    def fold_forward(index, carried):
        first_row = index * tok_rows
        key_piece = lax.dynamic_slice_in_dim(every_key, first_row, tok_rows, 0)
        value_piece = lax.dynamic_slice_in_dim(every_value, first_row, tok_rows, 0)
        return forward_step(carried, key_piece, value_piece, first_row, context)

    running = lax.fori_loop(0, cycle_size, fold_forward, start_state)
    row_max, row_total, accum = running
    attended = (accum / row_total[..., None]).astype(jnp.bfloat16)
    log_totals = row_max + jnp.log(row_total)
    branch_part = jnp.dot(attended.reshape(tok_rows, -1), w_out, preferred_element_type=jnp.float32)
    branch = sum_at_owner(branch_part, "mp", 1)
    x_first = y_first.astype(jnp.float32) - branch
    grad_out = lax.dot_general(
        grad_rows, w_out, (((1,), (1,)), ((), ())), preferred_element_type=jnp.float32
    )
    grad_out = grad_out.astype(jnp.bfloat16).reshape(tok_rows, kv_local, group_size, HEAD_DIM)
    deltas = jnp.sum(grad_out.astype(jnp.float32) * attended.astype(jnp.float32), axis=-1)
    back_context = (grad_out, log_totals, deltas)
    query_zero = jnp.zeros(head_shape + (HEAD_DIM,), jnp.float32)
    all_zero = jnp.zeros((tok_rows * cycle_size, key_flat.shape[1]), jnp.float32)

    def fold_backward(index, carried):
        query_grad, key_all, value_all = carried
        first_row = index * tok_rows
        key_piece = lax.dynamic_slice_in_dim(every_key, first_row, tok_rows, 0)
        value_piece = lax.dynamic_slice_in_dim(every_value, first_row, tok_rows, 0)
        key_part = lax.dynamic_slice_in_dim(key_all, first_row, tok_rows, 0)
        value_part = lax.dynamic_slice_in_dim(value_all, first_row, tok_rows, 0)
        query_grad, key_part, value_part = backward_step(
            (query_grad, key_part, value_part),
            key_piece,
            value_piece,
            first_row,
            context,
            back_context,
        )
        key_all = lax.dynamic_update_slice_in_dim(key_all, key_part, first_row, 0)
        value_all = lax.dynamic_update_slice_in_dim(value_all, value_part, first_row, 0)
        return (query_grad, key_all, value_all)

    query_grad, key_all, value_all = lax.fori_loop(
        0, cycle_size, fold_backward, (query_zero, all_zero, all_zero)
    )
    key_grad, value_grad = side_by_side_2((key_all, value_all), "seq", 0, 1)
    query_grad = query_grad.astype(jnp.bfloat16).reshape(tok_rows, -1)
    key_grad = key_grad.astype(jnp.bfloat16)
    value_grad = value_grad.astype(jnp.bfloat16)
    contract = (((1,), (1,)), ((), ()))
    normed_grad = lax.dot_general(query_grad, w_query, contract, preferred_element_type=jnp.float32)
    normed_grad = normed_grad + lax.dot_general(
        key_grad, w_key, contract, preferred_element_type=jnp.float32
    )
    normed_grad = normed_grad + lax.dot_general(
        value_grad, w_value, contract, preferred_element_type=jnp.float32
    )
    width = full_rows.shape[1]
    columns = x_second.shape[1]
    first_col = lax.axis_index("mp") * columns
    shared = sum_at_owner(normed_grad, "mp", 1)
    unit_share = lax.dynamic_slice_in_dim(unit_rows, first_col, columns, 1)
    gain_share = lax.dynamic_slice_in_dim(norm_gain, first_col, columns, 0)
    scaled = shared * gain_share
    partial_dot = jnp.sum(scaled * unit_share, axis=-1)
    total_dot = taken_together(partial_dot, "mp")
    input_grad = inverse_rms * (scaled - unit_share * (total_dot / width)[:, None])
    x_grad = grad_second.astype(jnp.float32) + input_grad
    return (x_first, x_grad)


def solution(mesh):
    placed = (
        P("seq", "mp"),
        P("seq", "mp"),
        P("seq", "mp"),
        P("seq", "mp"),
        P("seq"),
        P(),
        P(None, "mp"),
        P(None, "mp"),
        P(None, "mp"),
        P("mp", None),
    )
    return jax.shard_map(
        per_device,
        mesh=mesh,
        in_specs=placed,
        out_specs=(P("seq", "mp"), P("seq", "mp")),
        check_vma=False,
    )
```

profile of v0, /device:TPU:30, one launch (start us, length us, event | category | flops | bytes accessed | tf_op | source)
XLA Modules:
  0.0 756.3 jit_solution(6805836597228749920)
XLA Ops:
  7.2 2.4 pad_maximum_fusion.1
  9.7 51.0 %all-gather.3.cloned.1.call-done = bf16[512,4096]{1,0:T(8,128)(2,1)} async-done(((bf16[512,1024]{1,0:T(8,128)(2,1)}), bf16[512,4096]{1,0:T(8,128)(2,1)}) %all-gather.3.cloned.1.call-update) | async-done | bytes 4194320 | tf_op jit(solution)/shard_map/all_gather | solution.py:15
  60.7 2.2 fusion.46
  63.0 2.6 convolution_convert_fusion.1
  65.6 1.0 convolution_convert_fusion.2
  67.9 7.4 all-to-all-start
  75.6 4.2 fusion.49
  80.1 4.2 convolution_convert_fusion
  84.4 29.6 %all-gather.5.cloned.1.call-done = bf16[8192,256]{0,1:T(8,128)(2,1)} async-done(((bf16[256,256]{0,1:T(8,128)(2,1)}), bf16[8192,256]{0,1:T(8,128)(2,1)}) %all-gather.5.cloned.1.call-update) | async-done | bytes 4194320 | tf_op jit(solution)/shard_map/all_gather | solution.py:15
  114.0 4.6 fusion.55
  118.6 4.1 copy.53
  122.7 4.1 copy.60
  126.8 130.8 %while.34 = (s32[]{:T(128)}, f32[256,1,4]{0,2,1:T(4,128)S(1)}, f32[256,1,4]{0,2,1:T(4,128)S(1)}, f32[256,1,4,128]{0,3,2,1:T(8,128)S(1)}, s32[256]{0:T(256)S(1)},...) while((s32[]{:T(128)}, f32[256,1,4]{0,2,1:T(4,128)S(1)}, ...), condition=%wide.region_6.7_spmd, body=%wide.region_1.6_spmd.sunk | while | flops 472321280 | bytes 4925829 | solution.py:171
  243.3 3.3 conditional.4
  243.5 1.2 select_reduce_fusion
  244.9 1.7 fusion.1
  250.5 3.3 conditional.4
  250.6 1.2 select_reduce_fusion
  252.1 1.6 fusion.1
  258.4 2.2 broadcast_in_dim.93
  260.6 2.2 broadcast_in_dim.93.clone
  262.9 200.4 %while.35 = (s32[]{:T(128)}, f32[256,1,4,128]{0,3,2,1:T(8,128)S(1)}, f32[8192,128]{1,0:T(8,128)}, f32[8192,128]{1,0:T(8,128)}, s32[256]{0:T(256)S(1)}, /*index=5...) while((s32[]{:T(128)}, ...), condition=%wide.region_12.13_spmd, body=%wide.region_9.12_spmd.sunk | while | flops 337936640 | bytes 8736189 | solution.py:206
  442.1 4.3 conditional.5
  442.2 1.2 fusion.23
  443.5 1.1 fusion.25
  444.6 1.1 fusion.27
  452.3 4.3 conditional.5
  452.5 1.2 fusion.23
  453.7 1.1 fusion.25
  454.9 1.1 fusion.27
  463.3 7.2 pad_maximum_fusion
  470.6 6.5 copy.70
  477.1 5.4 convolution_bitcast_fusion.4
  482.5 5.1 all-to-all-start.1
  487.7 187.5 %reduce-scatter.2.cloned.1.call-done = f32[256,256]{1,0:T(8,128)} async-done(((f32[8192,256]{1,0:T(8,128)}), f32[256,256]{1,0:T(8,128)}) %reduce-scatter.2.cloned.1.call-update) | async-done | bytes 262160 | tf_op jit(solution)/shard_map/reduce_scatter | solution.py:51
  675.2 1.1 convert.4
  677.4 1.3 convolution_add_fusion
  679.5 2.3 copy.74
  681.8 4.8 all-to-all-start.2
  686.7 4.1 convert_multiply_fusion
  690.8 3.7 reduce_sum.68
  694.5 39.6 %all-to-all-done.2 = f32[4,256,1024]{2,1,0:T(8,128)} async-done(((f32[4,256,1024]{2,1,0:T(8,128)}), f32[4,256,1024]{2,1,0:T(8,128)}, u32[]{:S(2)}, u32[]{:S(2)}) %all-to-all-start.2) | async-done | bytes 4194336 | tf_op jit(solution)/shard_map/all_to_all | solution.py:45
  734.0 2.7 reduce_sum.71
  736.8 1.4 multiply_reduce_fusion
  738.8 3.2 all-to-all-start.3
  742.0 2.4 convert_subtract_fusion
  744.4 2.9 all-to-all-done.3
  747.3 2.5 multiply_add_fusion
  (544 shorter events, 204.2 us)
Async XLA Ops:
  7.2 58.4 %copy-start = (bf16[4096,128]{1,0:T(8,128)(2,1)S(1)}, bf16[4096,128]{1,0:T(8,128)(2,1)}, u32[]{:S(2)}) copy-start(bf16[4096,128]{1,0:T(8,128)(2,1)} %param.25) | copy-start | bytes 3145732
  7.2 55.8 %copy-start.8 = (f32[4096]{0:T(1024)S(1)}, f32[4096]{0:T(1024)}, u32[]{:S(2)}) copy-start(f32[4096]{0:T(1024)} %param.23) | copy-start | bytes 49156
  7.2 55.8 %copy-start.3 = (bf16[4096,128]{1,0:T(8,128)(2,1)S(1)}, bf16[4096,128]{1,0:T(8,128)(2,1)}, u32[]{:S(2)}) copy-start(bf16[4096,128]{1,0:T(8,128)(2,1)} %param.26) | copy-start | bytes 3145732
  7.2 53.5 %all-gather.3.cloned.1.call-start = ((), (), s32[]{:S(2)}) async-start(), calls=%async_computation.5 | async-start | bytes 5242880 | tf_op jit(solution)/shard_map/all_gather | solution.py:15
  9.6 104.3 %all-gather.5.cloned.1.call-start = ((), (), s32[]{:S(2)}) async-start(), calls=%async_computation.6 | async-start | bytes 4325376 | tf_op jit(solution)/shard_map/all_gather | solution.py:15
  60.7 4.8 copy-start.2
  65.6 1.7 copy-start.7
  67.9 58.8 %all-to-all-start = ((s32[32,1,256]{2,1,0:T(1,128)}), s32[32,1,256]{2,1,0:T(1,128)S(1)}, u32[]{:S(2)}, u32[]{:S(2)}) async-start(s32[32,1,256]{2,1,0:T(1,128)} %broadcast_in_dim.92), calls=%async_computation | async-start | bytes 65536 | tf_op jit(solution)/shard_map/all_to_all | solution.py:30
  75.3 599.9 %reduce-scatter.2.cloned.1.call-start = ((), (), s32[]{:S(2)}) async-start(), calls=%async_computation.7 | async-start | bytes 8650752 | tf_op jit(solution)/shard_map/reduce_scatter | solution.py:51
  470.6 6.5 copy-start.4
  482.5 199.3 %all-to-all-start.1 = ((f32[4,256,1024]{2,1,0:T(8,128)}), f32[4,256,1024]{2,1,0:T(8,128)}, u32[]{:S(2)}, u32[]{:S(2)}) async-start(f32[4,256,1024]{2,1,0:T(8,128)} %convolution_bitcast_fusion.4), calls=%async_computation.1 | async-start | bytes 8388608 | tf_op jit(solution)/shard_map/all_to_all | solution.py:45
  675.2 2.3 copy-start.1
  681.8 52.2 %all-to-all-start.2 = ((f32[4,256,1024]{2,1,0:T(8,128)}), f32[4,256,1024]{2,1,0:T(8,128)}, u32[]{:S(2)}, u32[]{:S(2)}) async-start(f32[4,256,1024]{2,1,0:T(8,128)} %bitcast.155), calls=%async_computation.3 | async-start | bytes 8388608 | tf_op jit(solution)/shard_map/all_to_all | solution.py:45
  694.5 47.6 %copy-start.5 = (bf16[256,1024]{1,0:T(8,128)(2,1)S(1)}, bf16[256,1024]{1,0:T(8,128)(2,1)}, u32[]{:S(2)}) copy-start(bf16[256,1024]{1,0:T(8,128)(2,1)} %param.18) | copy-start | bytes 1572868
  694.5 52.9 %copy-start.6 = (bf16[256,1024]{1,0:T(8,128)(2,1)S(1)}, bf16[256,1024]{1,0:T(8,128)(2,1)}, u32[]{:S(2)}) copy-start(bf16[256,1024]{1,0:T(8,128)(2,1)} %param.21) | copy-start | bytes 1572868
  738.8 8.5 %all-to-all-start.3 = ((f32[4,1,256]{2,1,0:T(1,128)}), f32[4,1,256]{2,1,0:T(1,128)S(1)}, u32[]{:S(2)}, u32[]{:S(2)}) async-start(f32[4,1,256]{2,1,0:T(1,128)} %broadcast_in_dim.94), calls=%async_computation.4 | async-start | bytes 8192 | tf_op jit(solution)/shard_map/all_to_all | solution.py:30
Sparse Core Ops, SparseCore 0:
  10.2 50.4 all-gather.2
  67.4 46.5 all-gather.4
  470.7 204.4 reduce-scatter.1
where the time goes:
time: 762 us; the launch traced here: 756 us
  waiting for transfers between devices  311 us (41%)
  local copies, waits for them, and re-layouts  224 us (29%)
  loops' own time  121 us (16%)
  matrix products  33.9 us (4%)
  other arithmetic  32.3 us (4%)
  starting transfers between devices  21 us (3%)
  between operations  14.1 us (2%)
    reduce_scatter x1, waiting for transfers between devices, side_by_side_2(): lax.psum_scatter(both, axis, scatter_dimension=dim, tiled=True)  187 us
    slice x192, local copies, waits for them, and re-layouts, key_meta(): needed = (first_key <= query_pos[-1]) & (key_doc[-1] >= query_doc[0])  108 us
    all_gather x2, waiting for transfers between devices, side_by_side(): whole, at, done = (lax.all_gather(both, axis, axis=dim, tiled=True), 0, [])  80.6 us
    another operation x1, loops' own time, per_device(): running = lax.fori_loop(0, cycle_size, fold_forward, start_state)  65.1 us
    another operation x1, loops' own time, per_device(): lax.fori_loop(0, cycle_size, fold_backward, (query_zero, all_zero, all_ze...  54.6 us
    all_to_all x2, waiting for transfers between devices, sum_at_owner(): tiles = lax.all_to_all(cut_along(value, dim, size), axis, 0, 0, tiled=True)  39.6 us
    dynamic_slice x32, local copies, waits for them, and re-layouts, fold_backward(): value_part = lax.dynamic_slice_in_dim(value_all, first_row, tok_rows, 0)  29.5 us
    dynamic_slice x32, local copies, waits for them, and re-layouts, fold_backward(): key_part = lax.dynamic_slice_in_dim(key_all, first_row, tok_rows, 0)  29.2 us
  transfers between devices with their start and end apart: 7, of which 5 were waited for; matrix products, arithmetic and copies ran while one was open for 7% of the time, Pallas kernels for 0%

commit v1 on v0

v1 whole, which is shorter than its diff:
```python
import jax
import jax.numpy as jnp
from jax import lax
from jax.experimental import pallas as pl
from jax.experimental.pallas import tpu as pltpu
from jax.sharding import PartitionSpec as P

HEAD = 128
EPSILON = 1e-05
MASKED = -1e30
SCALE = HEAD**-0.5
LOG2E = 1.4426950408889634
TOK = 256
HALF = TOK // 2
COLS = 1024
WIDTH = 4096
BAND = 17
ROWS_KV = TOK + 16
MIB = 1 << 20
NT = (((1,), (1,)), ((), ()))
TN = (((0,), (0,)), ((), ()))
F32 = jnp.float32
BF16 = jnp.bfloat16


def place():
    seq, mp = lax.axis_index("seq"), lax.axis_index("mp")
    core = lax.rem(seq, 2)
    x = lax.rem(lax.div(seq, 2), 4)
    y = lax.div(seq, 8)
    return seq, mp, y, x, core


def seq_of(y, x, core):
    return y * 8 + x * 2 + core


def plus(a, b, n=4):
    return lax.rem(a + (b + n) % n, n)


def remote(src, dst, sems, index, device):
    send, recv = sems
    return pltpu.make_async_remote_copy(
        src_ref=src,
        dst_ref=dst,
        send_sem=send.at[index],
        recv_sem=recv.at[index],
        device_id=device,
        device_id_type=pl.DeviceIdType.MESH,
    )


def greet(devices):
    barrier = pltpu.get_barrier_semaphore()
    for device in devices:
        pl.semaphore_signal(barrier, inc=1, device_id=device, device_id_type=pl.DeviceIdType.MESH)
    pl.semaphore_wait(barrier, len(devices))


class RingGather:
    def __init__(self, own, buf, slots, half, rows, sems, base, right, left):
        self.sems, self.base = sems, base
        me, l, r, o = slots
        a, b = pl.ds(0, half), pl.ds(half, rows - half)
        at = lambda slot, part: buf.at[slot, part]
        mk = lambda src, dst, i, dev: remote(src, dst, sems, base + i, dev)
        self.out = [
            mk(own.at[a], at(me, a), 0, right),
            mk(own.at[b], at(me, b), 1, right),
            mk(own.at[b], at(me, b), 2, left),
            mk(own.at[a], at(me, a), 3, left),
            mk(at(l, a), at(l, a), 4, right),
            mk(at(r, b), at(r, b), 5, left),
        ]
        self.inn = [
            mk(own.at[a], at(l, a), 0, right),
            mk(own.at[b], at(l, b), 1, right),
            mk(own.at[b], at(r, b), 2, left),
            mk(own.at[a], at(r, a), 3, left),
            mk(own.at[a], at(o, a), 4, right),
            mk(own.at[b], at(o, b), 5, left),
        ]

    def start(self):
        for i in (0, 2, 1, 3):
            self.out[i].start()

    def forward(self):
        self.inn[0].wait_recv()
        self.out[4].start()
        self.inn[2].wait_recv()
        self.out[5].start()

    def wait_left(self):
        self.inn[1].wait_recv()

    def wait_right(self):
        self.inn[3].wait_recv()

    def wait_far(self):
        self.inn[4].wait_recv()
        self.inn[5].wait_recv()

    def finish(self):
        for copy in self.out:
            copy.wait_send()


class RingReduce:
    def __init__(self, parts, relay, finals, slots, half, rows, sems, base, right, left):
        me, l, r, o = slots
        a, b = pl.ds(0, half), pl.ds(half, rows - half)
        self.parts, self.relay, self.finals = parts, relay, finals
        self.slots, self.a, self.b = slots, a, b
        mk = lambda src, dst, i, dev: remote(src, dst, sems, base + i, dev)
        self.out = [
            mk(parts(o, a), relay.at[0], 0, right),
            mk(parts(o, b), relay.at[1], 1, left),
            mk(parts(r, b), finals.at[0, b], 2, right),
            mk(parts(l, a), finals.at[1, a], 3, left),
            mk(parts(r, a), finals.at[0, a], 4, right),
            mk(parts(l, b), finals.at[1, b], 5, left),
        ]

    def start_far(self):
        self.out[0].start()
        self.out[1].start()

    def start_near(self):
        self.out[2].start()
        self.out[3].start()

    def forward(self):
        me, l, r, o = self.slots
        for i, slot, part in ((0, r, self.a), (1, l, self.b)):
            self.out[i].wait_recv()
            piece = self.parts(slot, part)
            piece[...] = (piece[...].astype(F32) + self.relay[i].astype(F32)).astype(BF16)
            self.out[4 + i].start()

    def wait_total(self):
        for i in (2, 3, 4, 5):
            self.out[i].wait_recv()
        me = self.slots[0]
        return lambda part: (
            self.parts(me, part)[...].astype(F32)
            + self.finals[0, part].astype(F32)
            + self.finals[1, part].astype(F32)
        )

    def finish(self):
        for copy in self.out:
            copy.wait_send()


def z_places(seq, mp):
    right, left, far = plus(mp, 1), plus(mp, -1), plus(mp, 2)
    return (mp, left, right, far), (seq, right), (seq, left), (seq, far)


def project_kernel(x_ref, gain_ref, docs_ref, wq_ref, wk_ref, wv_ref, q_ref, kvd_ref, inv_ref,
                   buf, weights, acc, scaled, mine, theirs, wsem, send, recv):
    seq, mp, y, x, core = place()
    slots, right, left, far = z_places(seq, mp)
    me, l, r, o = slots
    loads = []
    for n, slot in enumerate((me, l, r, o)):
        rows = pl.ds(pl.multiple_of(slot * COLS, COLS), COLS)
        group = []
        for i, (w, lo, hi) in enumerate(((wq_ref, 0, 512), (wk_ref, 512, 640), (wv_ref, 640, 768))):
            copy = pltpu.make_async_copy(w.at[rows], weights.at[rows, pl.ds(lo, hi - lo)], wsem.at[n, i])
            copy.start()
            group.append(copy)
        loads.append(group)
    values = x_ref[...].astype(F32)
    squares = jnp.sum(values * values, axis=-1, keepdims=True)
    mine[...] = jnp.broadcast_to(squares, (TOK, 128)).T[0:8, :]
    sems = (send, recv)
    greet([right, left, far])
    small = [
        remote(mine, theirs.at[i], sems, 6 + i, device) for i, device in enumerate((right, left, far))
    ]
    for copy in small:
        copy.start()
    ring = RingGather(x_ref, buf, slots, HALF, TOK, sems, 0, right, left)
    ring.start()
    kvd_ref[pl.ds(TOK, 16), :] = docs_ref[...]
    for copy in small:
        copy.wait_recv()
    squares = mine[...] + theirs[0] + theirs[1] + theirs[2]
    inverse = lax.rsqrt(squares[0:1, :] * (1.0 / WIDTH) + EPSILON)
    inv_ref[...] = jnp.broadcast_to(inverse, (128, TOK)).T

    def fold(n, slot, block):
        for copy in loads[n]:
            copy.wait()
        scaled[...] = (block[...].astype(F32) * inv_ref[:, 0:1] * gain_ref[pl.ds(slot, 1), :]).astype(BF16)
        rows = pl.ds(pl.multiple_of(slot * COLS, COLS), COLS)

        def column(i, carry):
            cols = pl.ds(pl.multiple_of(i * 256, 256), 256)
            term = jnp.dot(scaled[...], weights[rows, cols], preferred_element_type=F32)
            if n == 0:
                acc[:, cols] = term
            else:
                acc[:, cols] += term
            return carry

        lax.fori_loop(0, 3, column, 0)

    fold(0, me, x_ref)
    ring.forward()
    ring.wait_left()
    fold(1, l, buf.at[l])
    ring.wait_right()
    fold(2, r, buf.at[r])
    ring.wait_far()
    fold(3, o, buf.at[o])
    q_ref[...] = acc[:, pl.ds(0, 512)].astype(BF16)
    kvd_ref[pl.ds(0, TOK), :] = acc[:, pl.ds(512, 256)].astype(BF16)
    for copy in small:
        copy.wait_send()
    ring.finish()


VM = pl.BlockSpec(memory_space=pltpu.VMEM)
ANY = pl.BlockSpec(memory_space=pl.ANY)
DMA = pltpu.SemaphoreType.DMA


def project(x, gain, docs, w_query, w_key, w_value):
    return pl.pallas_call(
        project_kernel,
        name="project",
        out_shape=(
            jax.ShapeDtypeStruct((TOK, 512), BF16),
            jax.ShapeDtypeStruct((ROWS_KV, 256), BF16),
            jax.ShapeDtypeStruct((TOK, 128), F32),
        ),
        in_specs=[VM, VM, VM, ANY, ANY, ANY],
        out_specs=(VM, VM, VM),
        scratch_shapes=[
            pltpu.VMEM((4, TOK, COLS), BF16),
            pltpu.VMEM((WIDTH, 768), BF16),
            pltpu.VMEM((TOK, 768), F32),
            pltpu.VMEM((TOK, COLS), BF16),
            pltpu.VMEM((8, TOK), F32),
            pltpu.VMEM((3, 8, TOK), F32),
            DMA((4, 3)),
            DMA((9,)),
            DMA((9,)),
        ],
        compiler_params=pltpu.CompilerParams(
            collective_id=0, has_side_effects=True, vmem_limit_bytes=24 * MIB
        ),
    )(x, gain, docs, w_query, w_key, w_value)


def band_kernel(kvd_ref, g_ref, w_ref, kvb_ref, go_ref, buf, weights, acc, wsem, osem,
                zsend, zrecv, send, recv):
    seq, mp, y, x, core = place()
    slots, zright, zleft, zfar = z_places(seq, mp)
    me, l, r, o = slots
    loads = []
    for n, slot in enumerate((me, l, r, o)):
        cols = pl.ds(pl.multiple_of(slot * COLS, COLS), COLS)
        copy = pltpu.make_async_copy(w_ref.at[:, cols], weights.at[slot], wsem.at[n])
        copy.start()
        loads.append(copy)
    xr, xl, xo = plus(x, 1), plus(x, -1), plus(x, 2)
    up, down = (seq_of(plus(y, 1), x, core), mp), (seq_of(plus(y, -1), x, core), mp)
    right, left = (seq_of(y, xr, core), mp), (seq_of(y, xl, core), mp)
    partner = (seq_of(y, x, 1 - core), mp)
    own_copy = pltpu.make_async_copy(kvd_ref, kvb_ref.at[seq], osem.at[0])
    own_copy.start()
    greet([up, down, right, left, partner, zright, zleft])
    sems = (send, recv)
    zring = RingGather(g_ref, buf, slots, HALF, TOK, (zsend, zrecv), 0, zright, zleft)
    rows = [plus(y, -k) for k in range(3)]
    rings, across, across_in = [], [], []
    for k in range(3):
        at = [seq_of(rows[k], column, core) for column in (x, xl, xr, xo)]
        own = kvd_ref if k == 0 else kvb_ref.at[at[0]]
        rings.append(RingGather(own, kvb_ref, at, 128, ROWS_KV, sems, 6 * k, right, left))
        twin = [seq_of(rows[k], column, 1 - core) for column in (x, xl, xr, xo)]
        out, inn = [], []
        for n in range(4):
            src = kvd_ref if k == 0 and n == 0 else kvb_ref.at[at[n]]
            out.append(remote(src, kvb_ref.at[at[n]], sems, 18 + 4 * k + n, partner))
            inn.append(remote(src, kvb_ref.at[twin[n]], sems, 18 + 4 * k + n, partner))
        across.append(out)
        across_in.append(inn)
    b1, b2 = seq_of(rows[1], x, core), seq_of(rows[2], x, core)
    up_own = remote(kvd_ref, kvb_ref.at[seq], sems, 30, up)
    in_own = remote(kvd_ref, kvb_ref.at[b1], sems, 30, up)
    up_next = remote(kvb_ref.at[b1], kvb_ref.at[b1], sems, 31, up)
    in_next = remote(kvb_ref.at[b1], kvb_ref.at[b2], sems, 31, up)

    up_own.start()
    rings[0].start()
    zring.start()
    across[0][0].start()

    def fold(n, slot, block):
        loads[n].wait()
        term = lax.dot_general(block[...], weights[slot], NT, preferred_element_type=F32)
        if n == 0:
            acc[...] = term
        else:
            acc[...] += term

    rings[0].forward()
    in_own.wait_recv()
    up_next.start()
    rings[1].start()
    across[1][0].start()
    fold(0, me, g_ref)
    in_next.wait_recv()
    rings[2].start()
    across[2][0].start()
    rings[1].forward()
    zring.forward()
    for k in range(3):
        if k == 2:
            rings[2].forward()
        rings[k].wait_left()
        across[k][1].start()
        rings[k].wait_right()
        across[k][2].start()
    zring.wait_left()
    fold(1, l, buf.at[l])
    zring.wait_right()
    fold(2, r, buf.at[r])
    for k in range(3):
        rings[k].wait_far()
        across[k][3].start()
    zring.wait_far()
    fold(3, o, buf.at[o])
    go_ref[...] = acc[...].astype(BF16)
    own_copy.wait()
    for k in range(3):
        for n in range(4):
            across_in[k][n].wait_recv()
    up_own.wait_send()
    up_next.wait_send()
    zring.finish()
    for k in range(3):
        rings[k].finish()
        for n in range(4):
            across[k][n].wait_send()


def band(kvd, g, w_out):
    return pl.pallas_call(
        band_kernel,
        name="band",
        out_shape=(
            jax.ShapeDtypeStruct((32, ROWS_KV, 256), BF16),
            jax.ShapeDtypeStruct((TOK, 512), BF16),
        ),
        in_specs=[VM, VM, ANY],
        out_specs=(VM, VM),
        scratch_shapes=[
            pltpu.VMEM((4, TOK, COLS), BF16),
            pltpu.VMEM((4, 512, COLS), BF16),
            pltpu.VMEM((TOK, 512), F32),
            DMA((4,)),
            DMA((1,)),
            DMA((6,)),
            DMA((6,)),
            DMA((32,)),
            DMA((32,)),
        ],
        compiler_params=pltpu.CompilerParams(
            collective_id=1, has_side_effects=True, vmem_limit_bytes=24 * MIB
        ),
    )(kvd, g, w_out)


def attention_kernel(q_ref, kvb_ref, go_ref, docs_ref, att_ref, dq_ref, dkv_ref,
                     s_buf, p_buf, ka_buf, qt, qs, dot_buf, do_buf, o_acc, dq_acc, m_buf, l_buf, li_buf):
    seq = lax.axis_index("seq")
    blocks = jnp.minimum(seq, BAND - 1) + 1
    heads = [pl.ds(h * TOK, TOK) for h in range(4)]

    def clear(i, carry):
        dkv_ref[i] = jnp.zeros((TOK, 256), BF16)
        return carry

    lax.fori_loop(0, 32, clear, 0)
    for h in range(4):
        piece = q_ref[:, pl.ds(h * HEAD, HEAD)]
        qs[heads[h], :] = piece
        qt[pl.ds(0, HEAD), heads[h]] = piece.astype(F32).T.astype(BF16)
    docs = docs_ref[pl.ds(0, 8), :].astype(F32)[0:1, :]
    number = lax.broadcasted_iota(jnp.int32, (HEAD, TOK), 0).astype(F32)
    other = jnp.where(number == docs, 0.0, MASKED).astype(BF16)
    for h in range(4):
        qt[pl.ds(HEAD, HEAD), heads[h]] = other
    m_buf[...] = jnp.full(m_buf.shape, MASKED, F32)
    l_buf[...] = jnp.zeros(l_buf.shape, F32)
    o_acc[...] = jnp.zeros(o_acc.shape, F32)
    dq_acc[...] = jnp.zeros(dq_acc.shape, F32)

    def score(j, diagonal):
        b = seq - j
        key_docs = kvb_ref[b, pl.ds(TOK, 16), :].astype(F32)[0:1, :]
        same = jnp.where(number == key_docs, 1.0, 0.0)
        ka_buf[j, :, pl.ds(0, HEAD)] = kvb_ref[b, pl.ds(0, TOK), pl.ds(0, HEAD)]
        ka_buf[j, :, pl.ds(HEAD, HEAD)] = same.T.astype(BF16)
        for h in range(4):
            s = jnp.dot(ka_buf[j], qt[:, heads[h]], preferred_element_type=F32)
            if diagonal:
                key_at = lax.broadcasted_iota(jnp.int32, (TOK, TOK), 0)
                query_at = lax.broadcasted_iota(jnp.int32, (TOK, TOK), 1)
                s = jnp.where(key_at <= query_at, s, MASKED)
            s_buf[j, :, heads[h]] = s
            m_buf[:, heads[h]] = jnp.maximum(m_buf[:, heads[h]], s.reshape(TOK // 8, 8, TOK).max(axis=0))

    score(0, True)

    def score_step(j, carry):
        score(j, False)
        return carry

    lax.fori_loop(1, blocks, score_step, 0)
    top = jnp.max(m_buf[...], axis=0, keepdims=True)
    m_buf[...] = jnp.broadcast_to(top, m_buf.shape)

    def mix_step(j, carry):
        b = seq - j
        values = kvb_ref[b, pl.ds(0, TOK), pl.ds(HEAD, HEAD)]
        for h in range(4):
            s = s_buf[j, :, heads[h]]
            p = jnp.exp2((s - m_buf[0:1, heads[h]]) * (SCALE * LOG2E))
            l_buf[:, heads[h]] += p.reshape(TOK // 8, 8, TOK).sum(axis=0)
            p_buf[j, :, heads[h]] = p.astype(BF16)
            o_acc[:, heads[h]] += lax.dot_general(
                values, p.astype(BF16), TN, preferred_element_type=F32
            )
        return carry

    lax.fori_loop(0, blocks, mix_step, 0)
    inverse = 1.0 / jnp.sum(l_buf[...], axis=0, keepdims=True)
    li_buf[...] = jnp.broadcast_to(inverse, (8, 1024))
    for h in range(4):
        mixed = (o_acc[:, heads[h]] * inverse[:, h * TOK : (h + 1) * TOK]).astype(BF16).astype(F32)
        att_ref[:, pl.ds(h * HEAD, HEAD)] = mixed.T.astype(BF16)
        grad = go_ref[:, pl.ds(h * HEAD, HEAD)].astype(F32).T
        dot_buf[:, heads[h]] = grad.astype(BF16)
        do_buf[heads[h], :] = grad.T.astype(BF16)
        l_buf[:, heads[h]] = jnp.broadcast_to(jnp.sum(grad * mixed, axis=0, keepdims=True), (8, TOK))

    def back_step(j, carry):
        b = seq - j
        values = kvb_ref[b, pl.ds(0, TOK), pl.ds(HEAD, HEAD)]
        keys = kvb_ref[b, pl.ds(0, TOK), pl.ds(0, HEAD)]
        key_grad = jnp.zeros((TOK, HEAD), F32)
        value_grad = jnp.zeros((TOK, HEAD), F32)
        for h in range(4):
            s = s_buf[j, :, heads[h]]
            pf = jnp.exp2((s - m_buf[0:1, heads[h]]) * (SCALE * LOG2E)) * li_buf[0:1, heads[h]]
            p = pf.astype(BF16)
            dp = jnp.dot(values, dot_buf[:, heads[h]], preferred_element_type=F32)
            ds = (pf * (dp - l_buf[0:1, heads[h]])).astype(BF16)
            value_grad += jnp.dot(p, do_buf[heads[h], :], preferred_element_type=F32)
            key_grad += jnp.dot(ds, qs[heads[h], :], preferred_element_type=F32)
            dq_acc[:, heads[h]] += lax.dot_general(keys, ds, TN, preferred_element_type=F32)
        dkv_ref[b, :, pl.ds(0, HEAD)] = (key_grad * SCALE).astype(BF16)
        dkv_ref[b, :, pl.ds(HEAD, HEAD)] = value_grad.astype(BF16)
        return carry

    lax.fori_loop(0, blocks, back_step, 0)
    for h in range(4):
        dq_ref[:, pl.ds(h * HEAD, HEAD)] = (dq_acc[:, heads[h]] * SCALE).T.astype(BF16)


def attention(q, kvb, go, docs):
    return pl.pallas_call(
        attention_kernel,
        name="attention",
        out_shape=(
            jax.ShapeDtypeStruct((TOK, 512), BF16),
            jax.ShapeDtypeStruct((TOK, 512), BF16),
            jax.ShapeDtypeStruct((32, TOK, 256), BF16),
        ),
        in_specs=[VM] * 4,
        out_specs=(VM, VM, VM),
        scratch_shapes=[
            pltpu.VMEM((BAND, TOK, 1024), F32),
            pltpu.VMEM((BAND, TOK, 1024), BF16),
            pltpu.VMEM((BAND, TOK, 256), BF16),
            pltpu.VMEM((256, 1024), BF16),
            pltpu.VMEM((1024, HEAD), BF16),
            pltpu.VMEM((HEAD, 1024), BF16),
            pltpu.VMEM((1024, HEAD), BF16),
            pltpu.VMEM((HEAD, 1024), F32),
            pltpu.VMEM((HEAD, 1024), F32),
            pltpu.VMEM((8, 1024), F32),
            pltpu.VMEM((8, 1024), F32),
            pltpu.VMEM((8, 1024), F32),
        ],
        compiler_params=pltpu.CompilerParams(vmem_limit_bytes=56 * MIB),
    )(q, kvb, go, docs)


def collect_kernel(dkv_ref, att_ref, w_ref, grad_ref, branch_ref,
                   twin, sums, xrelay, xfinal, ynear, yown, weights, parts, zrelay, zfinal,
                   wsem, send, recv, zsend, zrecv):
    seq, mp, y, x, core = place()
    slots, zright, zleft, zfar = z_places(seq, mp)
    me, l, r, o = slots
    loads = []
    for n, slot in enumerate((o, r, l, me)):
        cols = pl.ds(pl.multiple_of(slot * COLS, COLS), COLS)
        copy = pltpu.make_async_copy(w_ref.at[:, cols], weights.at[slot], wsem.at[n])
        copy.start()
        loads.append(copy)
    xr, xl, xo = plus(x, 1), plus(x, -1), plus(x, 2)
    up, down = (seq_of(plus(y, 1), x, core), mp), (seq_of(plus(y, -1), x, core), mp)
    right, left = (seq_of(y, xr, core), mp), (seq_of(y, xl, core), mp)
    partner = (seq_of(y, x, 1 - core), mp)
    greet([up, down, right, left, partner, zright, zleft])
    sems = (send, recv)
    order = (2, 1, 0)
    rows = [plus(y, -k) for k in range(3)]
    across = [
        remote(dkv_ref.at[rows[k], :, 1 - core], twin.at[k], sems, k, partner) for k in range(3)
    ]
    for k in order:
        across[k].start()

    def term(n, slot):
        loads[n].wait()
        parts[slot] = jnp.dot(att_ref[...], weights[slot], preferred_element_type=F32).astype(BF16)

    zring = RingReduce(
        lambda slot, part: parts.at[slot, part], zrelay, zfinal, slots, HALF, TOK,
        (zsend, zrecv), 0, zright, zleft,
    )
    term(0, o)
    zring.start_far()
    rings = []
    for k in range(3):
        rings.append(
            RingReduce(
                lambda slot, part, k=k: sums.at[k, slot, part],
                xrelay.at[k], xfinal.at[k], (x, xl, xr, xo), HALF, TOK, sems, 3 + 6 * k, right, left,
            )
        )

    def open_ring(k):
        across[k].wait_recv()

        def add(i, carry):
            mine = dkv_ref[rows[k], i, core].astype(F32)
            sums[k, i] = (mine + twin[k, i].astype(F32)).astype(BF16)
            return carry

        lax.fori_loop(0, 4, add, 0)
        rings[k].start_far()
        rings[k].start_near()

    whole = pl.ds(0, TOK)
    open_ring(2)
    term(1, r)
    term(2, l)
    zring.start_near()
    open_ring(1)
    rings[2].forward()
    open_ring(0)
    rings[1].forward()
    term(3, me)
    far_up = remote(yown.at[0], ynear.at[0], sems, 21, down)
    near_up = remote(yown.at[1], ynear.at[1], sems, 22, down)
    zring.forward()
    yown[0] = rings[2].wait_total()(whole).astype(BF16)
    far_up.start()
    rings[0].forward()
    total = rings[1].wait_total()(whole)
    far_up.wait_recv()
    yown[1] = (total + ynear[0].astype(F32)).astype(BF16)
    near_up.start()
    total = rings[0].wait_total()(whole)
    near_up.wait_recv()
    grad_ref[...] = (total + ynear[1].astype(F32)).astype(BF16)
    total = zring.wait_total()
    for part in (pl.ds(0, HALF), pl.ds(HALF, HALF)):
        branch_ref[part, :] = total(part)
    for copy in across + [far_up, near_up]:
        copy.wait_send()
    for ring in rings + [zring]:
        ring.finish()


def collect(dkv, att, w_out):
    return pl.pallas_call(
        collect_kernel,
        name="collect",
        out_shape=(
            jax.ShapeDtypeStruct((TOK, 256), BF16),
            jax.ShapeDtypeStruct((TOK, COLS), F32),
        ),
        in_specs=[VM, VM, ANY],
        out_specs=(VM, VM),
        scratch_shapes=[
            pltpu.VMEM((3, 4, TOK, 256), BF16),
            pltpu.VMEM((3, 4, TOK, 256), BF16),
            pltpu.VMEM((3, 2, HALF, 256), BF16),
            pltpu.VMEM((3, 2, TOK, 256), BF16),
            pltpu.VMEM((2, TOK, 256), BF16),
            pltpu.VMEM((2, TOK, 256), BF16),
            pltpu.VMEM((4, 512, COLS), BF16),
            pltpu.VMEM((4, TOK, COLS), BF16),
            pltpu.VMEM((2, HALF, COLS), BF16),
            pltpu.VMEM((2, TOK, COLS), BF16),
            DMA((4,)),
            DMA((23,)),
            DMA((23,)),
            DMA((6,)),
            DMA((6,)),
        ],
        compiler_params=pltpu.CompilerParams(
            collective_id=2, has_side_effects=True, vmem_limit_bytes=32 * MIB
        ),
    )(dkv, att, w_out)


def norm_kernel(q_ref, kvd_ref, dq_ref, dkv_ref, wq_ref, wk_ref, wv_ref, out_ref, dot_ref,
                weights, grads, parts, relay, final, mine, theirs, wsem, send, recv):
    seq, mp, y, x, core = place()
    slots, right, left, far = z_places(seq, mp)
    me, l, r, o = slots
    loads = []
    for n, slot in enumerate((o, r, l, me)):
        rows = pl.ds(pl.multiple_of(slot * COLS, COLS), COLS)
        group = []
        for i, (w, lo, hi) in enumerate(((wq_ref, 0, 512), (wk_ref, 512, 640), (wv_ref, 640, 768))):
            copy = pltpu.make_async_copy(w.at[rows], weights.at[rows, pl.ds(lo, hi - lo)], wsem.at[n, i])
            copy.start()
            group.append(copy)
        loads.append(group)
    grads[:, pl.ds(0, 512)] = dq_ref[...]
    grads[:, pl.ds(512, 256)] = dkv_ref[...]
    greet([right, left, far])
    sems = (send, recv)

    def term(n, slot):
        for copy in loads[n]:
            copy.wait()

        def column(i, carry):
            rows = pl.ds(pl.multiple_of(slot * COLS + i * 256, 256), 256)
            cols = pl.ds(pl.multiple_of(i * 256, 256), 256)
            piece = lax.dot_general(grads[...], weights[rows, :], NT, preferred_element_type=F32)
            parts[slot, :, cols] = piece.astype(BF16)
            return carry

        lax.fori_loop(0, 4, column, 0)

    ring = RingReduce(
        lambda slot, part: parts.at[slot, part], relay, final, slots, HALF, TOK, sems, 0, right, left
    )
    term(0, o)
    ring.start_far()
    term(1, r)
    term(2, l)
    ring.start_near()
    dots = jnp.sum(q_ref[...].astype(F32) * dq_ref[...].astype(F32), axis=-1, keepdims=True)
    dots += jnp.sum(
        kvd_ref[pl.ds(0, TOK), :].astype(F32) * dkv_ref[...].astype(F32), axis=-1, keepdims=True
    )
    mine[...] = jnp.broadcast_to(dots, (TOK, 128)).T[0:8, :]
    small = [
        remote(mine, theirs.at[i], sems, 6 + i, device) for i, device in enumerate((right, left, far))
    ]
    for copy in small:
        copy.start()
    term(3, me)
    ring.forward()
    for copy in small:
        copy.wait_recv()
    dot_ref[...] = mine[...] + theirs[0] + theirs[1] + theirs[2]
    total = ring.wait_total()
    for part in (pl.ds(0, HALF), pl.ds(HALF, HALF)):
        out_ref[part, :] = total(part)
    for copy in small:
        copy.wait_send()
    ring.finish()


def norm_grad(q, kvd, dq, dkv, w_query, w_key, w_value):
    return pl.pallas_call(
        norm_kernel,
        name="norm_grad",
        out_shape=(
            jax.ShapeDtypeStruct((TOK, COLS), F32),
            jax.ShapeDtypeStruct((8, TOK), F32),
        ),
        in_specs=[VM, VM, VM, VM, ANY, ANY, ANY],
        out_specs=(VM, VM),
        scratch_shapes=[
            pltpu.VMEM((WIDTH, 768), BF16),
            pltpu.VMEM((TOK, 768), BF16),
            pltpu.VMEM((4, TOK, COLS), BF16),
            pltpu.VMEM((2, HALF, COLS), BF16),
            pltpu.VMEM((2, TOK, COLS), BF16),
            pltpu.VMEM((8, TOK), F32),
            pltpu.VMEM((3, 8, TOK), F32),
            DMA((4, 3)),
            DMA((9,)),
            DMA((9,)),
        ],
        compiler_params=pltpu.CompilerParams(
            collective_id=3, has_side_effects=True, vmem_limit_bytes=24 * MIB
        ),
    )(q, kvd, dq, dkv, w_query, w_key, w_value)


def per_device(
    y_first, x_second, grad_first, grad_second, doc_ids, norm_gain, w_query, w_key, w_value, w_out
):
    mp = lax.axis_index("mp")
    docs = jnp.broadcast_to(doc_ids.astype(BF16)[None, :], (16, TOK))
    gains = norm_gain.reshape(4, COLS)
    q, kvd, inverse = project(x_second, gains, docs, w_query, w_key, w_value)
    kvb, go = band(kvd, grad_first, w_out)
    att, dq, dkv = attention(q, kvb, go, docs)
    dkv, branch = collect(dkv.reshape(4, 4, 2, TOK, 256), att, w_out)
    x_first = y_first.astype(F32) - branch
    shared, dots = norm_grad(q, kvd, dq, dkv, w_query, w_key, w_value)
    inverse = inverse[:, :1]
    unit = x_second.astype(F32) * inverse
    gain = lax.dynamic_slice_in_dim(gains, mp, 1, 0)
    mean = (dots[0] * (1.0 / WIDTH))[:, None]
    x_grad = grad_second.astype(F32) + inverse * (shared * gain - unit * mean)
    return (x_first, x_grad)


def solution(mesh):
    placed = (
        P("seq", "mp"),
        P("seq", "mp"),
        P("seq", "mp"),
        P("seq", "mp"),
        P("seq"),
        P(),
        P(None, "mp"),
        P(None, "mp"),
        P(None, "mp"),
        P("mp", None),
    )
    return jax.shard_map(
        per_device,
        mesh=mesh,
        in_specs=placed,
        out_specs=(P("seq", "mp"), P("seq", "mp")),
        check_vma=False,
    )
```

time: 762 us -> 148 us (0.19)
  waiting for transfers between devices: 311 us -> 0 us
  local copies, waits for them, and re-layouts: 224 us -> 12.8 us
  Pallas kernels: 0 us -> 129 us
  loops' own time: 121 us -> 0 us
  matrix products: 33.9 us -> 0 us
  other arithmetic: 32.3 us -> 2.38 us
  starting transfers between devices: 21 us -> 0 us
  between operations: 14.1 us -> 0.85 us
    reduce_scatter x1 -> x0, waiting for transfers between devices: 187 us -> none  [side_by_side_2(): lax.psum_scatter(both, axis, scatter_dimension=dim, tiled=True)]
    pallas_call x0 -> x5, Pallas kernels: none -> 129 us  [the longest x1 34.8 us: attention(): pl.pallas_call(attention_kernel, name='attention', out_shape=(jax.ShapeDt...]
    another operation x66 -> x0, loops' own time: 121 us -> none  [the longest x1 65.1 us: per_device(): running = lax.fori_loop(0, cycle_size, fold_forward, start_state)]
    slice x193 -> x1, local copies, waits for them, and re-layouts: 113 us -> 0.1 us  [per_device(): inverse = inverse[:, :1]]
    all_gather x2 -> x0, waiting for transfers between devices: 80.6 us -> none  [side_by_side(): whole, at, done = (lax.all_gather(both, axis, axis=dim, tiled=True), 0, [])]
    dynamic_slice x129 -> x1, local copies, waits for them, and re-layouts: 63.7 us -> 0.01 us  [per_device(): gain = lax.dynamic_slice_in_dim(gains, mp, 1, 0)]
    all_to_all x4 -> x0, waiting for transfers between devices: 42.4 us -> none  [the longest x2 39.6 us: sum_at_owner(): tiles = lax.all_to_all(cut_along(value, dim, size), axis, 0, 0, tiled=True)]
    dot_general x22 -> x0, matrix products: 33.9 us -> none  [the longest x1 5.44 us: per_device(): jnp.dot(attended.reshape(tok_rows, -1), w_out, preferred_element_type=jnp...]
  transfers between devices with their start and end apart: 7 -> 0, of which waited for: 5 -> 0; matrix products, arithmetic and copies ran while one was open for 7% -> 0% of each run, Pallas kernels for 0% -> 0%
where the time goes in v1:
time: 148 us; the launch traced here: 145 us
  Pallas kernels  129 us (87%)
  local copies, waits for them, and re-layouts  12.8 us (9%)
  other arithmetic  2.38 us (2%)
    pallas_call x1, Pallas kernels, attention(): pl.pallas_call(attention_kernel, name='attention', out_shape=(jax.ShapeDt...  34.8 us
    pallas_call x1, Pallas kernels, project(): pl.pallas_call(project_kernel, name='project', out_shape=(jax.ShapeDtypeS...  24.8 us
    pallas_call x1, Pallas kernels, norm_grad(): pl.pallas_call(norm_kernel, name='norm_grad', out_shape=(jax.ShapeDtypeSt...  23.6 us
    pallas_call x1, Pallas kernels, collect(): pl.pallas_call(collect_kernel, name='collect', out_shape=(jax.ShapeDtypeS...  23.2 us
    pallas_call x1, Pallas kernels, band(): pl.pallas_call(band_kernel, name='band', out_shape=(jax.ShapeDtypeStruct(...  23 us
    unnamed x40, local copies, waits for them, and re-layouts  11.9 us

profile of v1, /device:TPU:30, one launch (start us, length us, event | category | flops | bytes accessed | tf_op | source)
XLA Modules:
  0.0 145.4 jit_solution(8349196968082544234)
XLA Ops:
  0.6 0.7 convert_element_type.13
  1.3 0.0 copy-start.17
  1.3 0.7 reshape.18.gain_ref
  2.1 0.0 copy-start
  2.1 0.0 copy-start.1
  2.1 2.3 %copy-done.1 = bf16[4096,512]{1,0:T(8,128)(2,1)S(1)} copy-done((bf16[4096,512]{1,0:T(8,128)(2,1)S(1)}, bf16[4096,512]{1,0:T(8,128)(2,1)}, u32[]{:S(2)}) %copy-start.1) | copy-done | bytes 4194328
  4.4 0.0 copy-start.5
  4.4 1.4 copy-done.5
  5.8 0.0 copy-start.7
  5.8 1.2 copy-done.7
  7.0 0.0 copy-start.9
  7.0 1.0 copy-done.9
  8.1 0.0 copy-start.13
  8.1 24.8 %project.1 = (bf16[256,512]{1,0:T(8,128)(2,1)S(1)}, bf16[272,256]{1,0:T(8,128)(2,1)S(1)}, f32[256,128]{1,0:T(8,128)S(1)}) custom-call(bf16[256,1024]{1,0:T(8,128)(2,1)S(1)} %copy-done.9, f32[4,1024]{1,0:T(4,128)S(1)} %reshape.18.gain_ref, bf16[16,256]{1,0:T(8,128)(2,1)S(1)} %broadcast_in_dim.2.docs_ref, bf16[4096,512]{1,0:T(8,128)(2,1)S(1)} %copy-done.1, ...), custom_call_target="tpu_custom_call" | custom-call | tf_op jit(solution)/shard_map/project/pallas_call | solution.py:233
  32.9 0.0 copy-start.11
  32.9 0.1 slice_reduce_fusion
  33.0 0.0 copy-done
  33.0 0.0 copy-done.13
  33.0 23.0 %band.1 = (bf16[32,272,256]{2,1,0:T(8,128)(2,1)S(1)}, bf16[256,512]{1,0:T(8,128)(2,1)S(1)}) custom-call(bf16[272,256]{1,0:T(8,128)(2,1)S(1)} %get-tuple-element.15.kvd_ref, bf16[256,1024]{1,0:T(8,128)(2,1)S(1)} %copy-done.13, bf16[512,4096]{1,0:T(8,128)(2,1)S(1)} %copy-done), custom_call_target="tpu_custom_call" | custom-call | tf_op jit(solution)/shard_map/band/pallas_call | solution.py:355
  56.0 0.0 copy-done.17
  56.0 0.0 copy-done.11
  56.0 0.0 copy-start.3
  56.0 2.1 %copy-done.3 = bf16[32,272,256]{2,1,0:T(8,128)(2,1)} copy-done((bf16[32,272,256]{2,1,0:T(8,128)(2,1)}, bf16[32,272,256]{2,1,0:T(8,128)(2,1)S(1)}, u32[]{:S(2)}) %copy-start.3) | copy-done | bytes 4456472
  58.1 0.0 copy-start.16
  58.1 0.7 copy-done.16
  58.8 34.8 %attention.1 = (bf16[256,512]{1,0:T(8,128)(2,1)}, bf16[256,512]{1,0:T(8,128)(2,1)}, bf16[32,256,256]{2,1,0:T(8,128)(2,1)}) custom-call(bf16[256,512]{1,0:T(8,128)(2,1)} %copy-done.11, bf16[32,272,256]{2,1,0:T(8,128)(2,1)} %copy-done.3, bf16[256,512]{1,0:T(8,128)(2,1)} %copy-done.16, bf16[16,256]{1,0:T(8,128)(2,1)} %copy-done.17), custom_call_target="tpu_custom_call" | custom-call | tf_op jit(solution)/shard_map/attention/pallas_call | solution.py:480
  93.6 0.0 copy-start.4
  93.6 2.2 %copy-done.4 = bf16[32,256,256]{2,1,0:T(8,128)(2,1)S(1)} copy-done((bf16[32,256,256]{2,1,0:T(8,128)(2,1)S(1)}, bf16[32,256,256]{2,1,0:T(8,128)(2,1)}, u32[]{:S(2)}) %copy-start.4) | copy-done | bytes 4194328
  95.8 0.0 copy-start.15
  95.8 0.9 copy-done.15
  96.7 0.0 copy-start.2
  96.7 0.0 copy-start.6
  96.7 0.0 copy-start.8
  96.8 0.0 copy-start.14
  96.8 23.2 %collect.1 = (bf16[256,256]{1,0:T(8,128)(2,1)S(1)}, f32[256,1024]{1,0:T(8,128)S(1)}) custom-call(bf16[4,4,2,256,256]{4,3,2,1,0:T(8,128)(2,1)S(1)} %bitcast.3, bf16[256,512]{1,0:T(8,128)(2,1)S(1)} %copy-done.15, bf16[512,4096]{1,0:T(8,128)(2,1)S(1)} %copy-done), custom_call_target="tpu_custom_call" | custom-call | tf_op jit(solution)/shard_map/collect/pallas_call | solution.py:598
  120.0 0.0 copy-start.10
  120.0 0.0 copy-start.18
  120.0 0.0 copy-start.19
  120.0 0.0 copy-done.2
  120.0 0.0 copy-done.6
  120.0 0.0 copy-done.8
  120.0 0.0 copy-done.12
  120.1 0.0 copy-done.14
  120.1 23.6 %norm_grad.1 = (f32[256,1024]{1,0:T(8,128)S(1)}, f32[8,256]{1,0:T(8,128)S(1)}) custom-call(bf16[256,512]{1,0:T(8,128)(2,1)S(1)} %copy-done.12, bf16[272,256]{1,0:T(8,128)(2,1)S(1)} %get-tuple-element.15.kvd_ref, bf16[256,512]{1,0:T(8,128)(2,1)S(1)} %copy-done.14, bf16[256,256]{1,0:T(8,128)(2,1)S(1)} %get-tuple-element.23.dkv_ref, ...), custom_call_target="tpu_custom_call" | custom-call | tf_op jit(solution)/shard_map/norm_grad/pallas_call | solution.py:694
  143.7 0.0 copy-done.10
  143.7 0.0 copy-done.18
  143.7 0.0 copy-done.19
  143.7 1.7 %multiply_add_fusion = (f32[256,1024]{1,0:T(8,128)}, f32[256,1024]{1,0:T(8,128)}) fusion(bf16[256,1024]{1,0:T(8,128)(2,1)S(1)} %copy-done.10, f32[256,1024]{1,0:T(8,128)S(1)} %get-tuple-element.24, bf16[256,1024]{1,0:T(8,128)(2,1)S(1)} %copy-done.18, f32[256]{0:T(256)S(1)} %bitcast.5, f32[1024]{0:T(1024)S(1)} %bitcast.4, f32[256]{0:T(256)S(1)} %slice_reduce_fusion, ...), kind=kLoop, calls=%fused_computation | loop fusion | flops 2621440 | bytes 5773312 | tf_op jit(solution)/shard_map/add | solution.py:737
  (4 shorter events, 0.0 us)
Async XLA Ops:
  1.3 54.7 %copy-start.17 = (bf16[16,256]{1,0:T(8,128)(2,1)}, bf16[16,256]{1,0:T(8,128)(2,1)S(1)}, u32[]{:S(2)}) copy-start(bf16[16,256]{1,0:T(8,128)(2,1)S(1)} %broadcast_in_dim.2.docs_ref) | copy-start | bytes 24580
  2.1 30.9 %copy-start = (bf16[512,4096]{1,0:T(8,128)(2,1)S(1)}, bf16[512,4096]{1,0:T(8,128)(2,1)}, u32[]{:S(2)}) copy-start(bf16[512,4096]{1,0:T(8,128)(2,1)} %w_ref.3) | copy-start | bytes 12582916
  2.1 2.3 %copy-start.1 = (bf16[4096,512]{1,0:T(8,128)(2,1)S(1)}, bf16[4096,512]{1,0:T(8,128)(2,1)}, u32[]{:S(2)}) copy-start(bf16[4096,512]{1,0:T(8,128)(2,1)} %wq_ref.3) | copy-start | bytes 12582916
  4.4 1.4 copy-start.5
  5.8 1.2 copy-start.7
  7.0 1.0 copy-start.9
  8.1 24.9 %copy-start.13 = (bf16[256,1024]{1,0:T(8,128)(2,1)S(1)}, bf16[256,1024]{1,0:T(8,128)(2,1)}, u32[]{:S(2)}) copy-start(bf16[256,1024]{1,0:T(8,128)(2,1)} %g_ref.1) | copy-start | bytes 1572868
  32.9 23.1 %copy-start.11 = (bf16[256,512]{1,0:T(8,128)(2,1)}, bf16[256,512]{1,0:T(8,128)(2,1)S(1)}, u32[]{:S(2)}) copy-start(bf16[256,512]{1,0:T(8,128)(2,1)S(1)} %get-tuple-element.14.q_ref) | copy-start | bytes 786436
  56.0 2.1 %copy-start.3 = (bf16[32,272,256]{2,1,0:T(8,128)(2,1)}, bf16[32,272,256]{2,1,0:T(8,128)(2,1)S(1)}, u32[]{:S(2)}) copy-start(bf16[32,272,256]{2,1,0:T(8,128)(2,1)S(1)} %get-tuple-element.16.kvb_ref) | copy-start | bytes 13369348
  58.1 0.7 copy-start.16
  93.6 2.2 %copy-start.4 = (bf16[32,256,256]{2,1,0:T(8,128)(2,1)S(1)}, bf16[32,256,256]{2,1,0:T(8,128)(2,1)}, u32[]{:S(2)}) copy-start(bf16[32,256,256]{2,1,0:T(8,128)(2,1)} %get-tuple-element.18) | copy-start | bytes 12582916
  95.8 0.9 copy-start.15
  96.7 23.3 %copy-start.2 = (bf16[4096,512]{1,0:T(8,128)(2,1)S(1)}, bf16[4096,512]{1,0:T(8,128)(2,1)}, u32[]{:S(2)}) copy-start(bf16[4096,512]{1,0:T(8,128)(2,1)} %wq_ref.3) | copy-start | bytes 12582916
  96.7 23.3 %copy-start.6 = (bf16[4096,128]{1,0:T(8,128)(2,1)S(1)}, bf16[4096,128]{1,0:T(8,128)(2,1)}, u32[]{:S(2)}) copy-start(bf16[4096,128]{1,0:T(8,128)(2,1)} %wk_ref.3) | copy-start | bytes 3145732
  96.7 23.3 %copy-start.8 = (bf16[4096,128]{1,0:T(8,128)(2,1)S(1)}, bf16[4096,128]{1,0:T(8,128)(2,1)}, u32[]{:S(2)}) copy-start(bf16[4096,128]{1,0:T(8,128)(2,1)} %wv_ref.3) | copy-start | bytes 3145732
  96.8 23.3 %copy-start.12 = (bf16[256,512]{1,0:T(8,128)(2,1)S(1)}, bf16[256,512]{1,0:T(8,128)(2,1)}, u32[]{:S(2)}) copy-start(bf16[256,512]{1,0:T(8,128)(2,1)} %copy-done.11) | copy-start | bytes 786436
  96.8 23.3 %copy-start.14 = (bf16[256,512]{1,0:T(8,128)(2,1)S(1)}, bf16[256,512]{1,0:T(8,128)(2,1)}, u32[]{:S(2)}) copy-start(bf16[256,512]{1,0:T(8,128)(2,1)} %get-tuple-element.22.dq_ref) | copy-start | bytes 786436
  120.0 23.7 %copy-start.10 = (bf16[256,1024]{1,0:T(8,128)(2,1)S(1)}, bf16[256,1024]{1,0:T(8,128)(2,1)}, u32[]{:S(2)}) copy-start(bf16[256,1024]{1,0:T(8,128)(2,1)} %x_ref.1) | copy-start | bytes 1572868
  120.0 23.7 %copy-start.18 = (bf16[256,1024]{1,0:T(8,128)(2,1)S(1)}, bf16[256,1024]{1,0:T(8,128)(2,1)}, u32[]{:S(2)}) copy-start(bf16[256,1024]{1,0:T(8,128)(2,1)} %param.13) | copy-start | bytes 1572868
  120.0 23.7 %copy-start.19 = (bf16[256,1024]{1,0:T(8,128)(2,1)S(1)}, bf16[256,1024]{1,0:T(8,128)(2,1)}, u32[]{:S(2)}) copy-start(bf16[256,1024]{1,0:T(8,128)(2,1)} %param.10) | copy-start | bytes 1572868

commit v2 on v0

v2 whole, which is shorter than its diff:
```python
import jax
import jax.numpy as jnp
from jax import lax
from jax.experimental import pallas as pl
from jax.experimental.pallas import tpu as pltpu
from jax.sharding import PartitionSpec as P

HEAD = 128
EPSILON = 1e-05
MASKED = -1e30
SCALE = HEAD**-0.5
LOG2E = 1.4426950408889634
TOK = 256
HALF = TOK // 2
COLS = 1024
WIDTH = 4096
BAND = 17
ROWS_KV = TOK + 16
MIB = 1 << 20
NT = (((1,), (1,)), ((), ()))
TN = (((0,), (0,)), ((), ()))
F32 = jnp.float32
BF16 = jnp.bfloat16


def place():
    seq, mp = lax.axis_index("seq"), lax.axis_index("mp")
    core = lax.rem(seq, 2)
    x = lax.rem(lax.div(seq, 2), 4)
    y = lax.div(seq, 8)
    return seq, mp, y, x, core


def seq_of(y, x, core):
    return y * 8 + x * 2 + core


def plus(a, b, n=4):
    return lax.rem(a + (b + n) % n, n)


def remote(src, dst, sems, index, device):
    send, recv = sems
    return pltpu.make_async_remote_copy(
        src_ref=src,
        dst_ref=dst,
        send_sem=send.at[index],
        recv_sem=recv.at[index],
        device_id=device,
        device_id_type=pl.DeviceIdType.MESH,
    )


def greet(devices):
    barrier = pltpu.get_barrier_semaphore()
    for device in devices:
        pl.semaphore_signal(barrier, inc=1, device_id=device, device_id_type=pl.DeviceIdType.MESH)
    pl.semaphore_wait(barrier, len(devices))


class RingGather:
    def __init__(self, own, buf, slots, half, rows, sems, base, right, left):
        self.sems, self.base = sems, base
        me, l, r, o = slots
        a, b = pl.ds(0, half), pl.ds(half, rows - half)
        at = lambda slot, part: buf.at[slot, part]
        mk = lambda src, dst, i, dev: remote(src, dst, sems, base + i, dev)
        self.out = [
            mk(own.at[a], at(me, a), 0, right),
            mk(own.at[b], at(me, b), 1, right),
            mk(own.at[b], at(me, b), 2, left),
            mk(own.at[a], at(me, a), 3, left),
            mk(at(l, a), at(l, a), 4, right),
            mk(at(r, b), at(r, b), 5, left),
        ]
        self.inn = [
            mk(own.at[a], at(l, a), 0, right),
            mk(own.at[b], at(l, b), 1, right),
            mk(own.at[b], at(r, b), 2, left),
            mk(own.at[a], at(r, a), 3, left),
            mk(own.at[a], at(o, a), 4, right),
            mk(own.at[b], at(o, b), 5, left),
        ]

    def start(self):
        for i in (0, 2, 1, 3):
            self.out[i].start()

    def forward(self):
        self.inn[0].wait_recv()
        self.out[4].start()
        self.inn[2].wait_recv()
        self.out[5].start()

    def wait_left(self):
        self.inn[1].wait_recv()

    def wait_right(self):
        self.inn[3].wait_recv()

    def wait_far(self):
        self.inn[4].wait_recv()
        self.inn[5].wait_recv()

    def finish(self):
        for copy in self.out:
            copy.wait_send()


class RingReduce:
    def __init__(self, parts, relay, finals, slots, half, rows, sems, base, right, left):
        me, l, r, o = slots
        a, b = pl.ds(0, half), pl.ds(half, rows - half)
        self.parts, self.relay, self.finals = parts, relay, finals
        self.slots, self.a, self.b = slots, a, b
        mk = lambda src, dst, i, dev: remote(src, dst, sems, base + i, dev)
        self.out = [
            mk(parts(o, a), relay.at[0], 0, right),
            mk(parts(o, b), relay.at[1], 1, left),
            mk(parts(r, b), finals.at[0, b], 2, right),
            mk(parts(l, a), finals.at[1, a], 3, left),
            mk(parts(r, a), finals.at[0, a], 4, right),
            mk(parts(l, b), finals.at[1, b], 5, left),
        ]

    def start_far(self):
        self.out[0].start()
        self.out[1].start()

    def start_near(self):
        self.out[2].start()
        self.out[3].start()

    def forward(self):
        me, l, r, o = self.slots
        for i, slot, part in ((0, r, self.a), (1, l, self.b)):
            self.out[i].wait_recv()
            piece = self.parts(slot, part)
            piece[...] = (piece[...].astype(F32) + self.relay[i].astype(F32)).astype(BF16)
            self.out[4 + i].start()

    def wait_total(self):
        for i in (2, 3, 4, 5):
            self.out[i].wait_recv()
        me = self.slots[0]
        return lambda part: (
            self.parts(me, part)[...].astype(F32)
            + self.finals[0, part].astype(F32)
            + self.finals[1, part].astype(F32)
        )

    def finish(self):
        for copy in self.out:
            copy.wait_send()


def z_places(seq, mp):
    right, left, far = plus(mp, 1), plus(mp, -1), plus(mp, 2)
    return (mp, left, right, far), (seq, right), (seq, left), (seq, far)


VM = pl.BlockSpec(memory_space=pltpu.VMEM)
ANY = pl.BlockSpec(memory_space=pl.ANY)
DMA = pltpu.SemaphoreType.DMA


def block_kernel(x_ref, g_ref, docs_ref, gain_ref, wq_ref, wk_ref, wv_ref, wo_ref,
                 branch_ref, out_ref, dot_ref, inv_ref,
                 x_buf, g_buf, weights, w_out, acc, go_acc, scaled, mine, theirs, kvb, s_buf, ka, qt, qs,
                 dot_buf, do_buf, o_acc, dq_acc, m_buf, m_run, l_buf, li_buf, d_buf, att, dkv, twin, sums,
                 xrelay, xfinal, ynear, yown, brelay, bfinal, nrelay, nfinal, grads,
                 lsem, zsend, zrecv, send, recv):
    seq, mp, y, x, core = place()
    slots, zright, zleft, zfar = z_places(seq, mp)
    me, l, r, o = slots
    zsems, sems = (zsend, zrecv), (send, recv)
    xr, xl, xo = plus(x, 1), plus(x, -1), plus(x, 2)
    up, down = (seq_of(plus(y, 1), x, core), mp), (seq_of(plus(y, -1), x, core), mp)
    right, left = (seq_of(y, xr, core), mp), (seq_of(y, xl, core), mp)
    partner = (seq_of(y, x, 1 - core), mp)
    rows = [plus(y, -k) for k in range(3)]
    heads = [pl.ds(h * TOK, TOK) for h in range(4)]
    whole = pl.ds(0, TOK)

    x_load = pltpu.make_async_copy(x_ref, x_buf.at[me], lsem.at[0])
    x_load.start()
    loads = []
    for n, slot in enumerate((me, l, r, o)):
        at = pl.ds(pl.multiple_of(slot * COLS, COLS), COLS)
        group = []
        for i, (w, lo, hi) in enumerate(((wq_ref, 0, 512), (wk_ref, 512, 640), (wv_ref, 640, 768))):
            copy = pltpu.make_async_copy(w.at[at], weights.at[at, pl.ds(lo, hi - lo)], lsem.at[1 + 3 * n + i])
            copy.start()
            group.append(copy)
        loads.append(group)
    g_load = pltpu.make_async_copy(g_ref, g_buf.at[me], lsem.at[13])
    g_load.start()
    w_loads = []
    for n, slot in enumerate((me, l, r, o)):
        cols = pl.ds(pl.multiple_of(slot * COLS, COLS), COLS)
        copy = pltpu.make_async_copy(wo_ref.at[:, cols], w_out.at[slot], lsem.at[14 + n])
        copy.start()
        w_loads.append(copy)

    x_load.wait()
    values = x_buf[me].astype(F32)
    squares = jnp.sum(values * values, axis=-1, keepdims=True)
    mine[0] = jnp.broadcast_to(squares, (TOK, 128)).T[0:8, :]
    greet([up, down, right, left, partner, zright, zleft, zfar])

    def exchange(which, base):
        return [
            remote(mine.at[which], theirs.at[which, i], zsems, base + i, device)
            for i, device in enumerate((zright, zleft, zfar))
        ]

    small = exchange(0, 6)
    for copy in small:
        copy.start()
    x_ring = RingGather(x_buf.at[me], x_buf, slots, HALF, TOK, zsems, 0, zright, zleft)
    x_ring.start()
    docs = docs_ref[...].astype(F32)
    kvb[seq, pl.ds(TOK, 16), :] = jnp.broadcast_to(docs, (16, TOK)).astype(BF16)

    def clear(i, carry):
        for k in range(3):
            for c in range(2):
                dkv[k, i, c] = jnp.zeros((TOK, 256), BF16)
        return carry

    lax.fori_loop(0, 4, clear, 0)
    for copy in small:
        copy.wait_recv()
    squares = mine[0] + theirs[0, 0] + theirs[0, 1] + theirs[0, 2]
    inverse = lax.rsqrt(squares[0:1, :] * (1.0 / WIDTH) + EPSILON)
    inv_ref[...] = jnp.broadcast_to(inverse, (128, TOK)).T

    def column(n, slot, i):
        at = pl.ds(pl.multiple_of(slot * COLS, COLS), COLS)
        cols = pl.ds(i * 256, 256)
        term = jnp.dot(scaled[...], weights[at, cols], preferred_element_type=F32)
        acc[:, cols] = term if n == 0 else acc[:, cols] + term

    def scale_rows(n, slot):
        for copy in loads[n]:
            copy.wait()
        gain = gain_ref[:, pl.ds(pl.multiple_of(slot * COLS, COLS), COLS)]
        scaled[...] = (x_buf[slot].astype(F32) * inv_ref[:, 0:1] * gain).astype(BF16)

    def fold(n, slot):
        scale_rows(n, slot)
        for i in range(3):
            column(n, slot, i)

    def fold_grad(n, slot):
        w_loads[n].wait()
        term = lax.dot_general(g_buf[slot], w_out[slot], NT, preferred_element_type=F32)
        go_acc[...] = term if n == 0 else go_acc[...] + term

    g_ring = RingGather(g_buf.at[me], g_buf, slots, HALF, TOK, zsems, 9, zright, zleft)
    fold(0, me)
    x_ring.forward()
    g_load.wait()
    g_ring.start()
    fold_grad(0, me)
    x_ring.wait_left()
    fold(1, l)
    x_ring.wait_right()
    fold(2, r)
    x_ring.wait_far()
    scale_rows(3, o)
    column(3, o, 2)
    kvb[seq, whole, :] = acc[:, pl.ds(512, 256)].astype(BF16)

    rings, across, across_in = [], [], []
    for k in range(3):
        at = [seq_of(rows[k], column_, core) for column_ in (x, xl, xr, xo)]
        rings.append(RingGather(kvb.at[at[0]], kvb, at, 128, ROWS_KV, sems, 6 * k, right, left))
        there = [seq_of(rows[k], column_, 1 - core) for column_ in (x, xl, xr, xo)]
        across.append(
            [remote(kvb.at[at[n]], kvb.at[at[n]], sems, 18 + 4 * k + n, partner) for n in range(4)]
        )
        across_in.append(
            [remote(kvb.at[at[n]], kvb.at[there[n]], sems, 18 + 4 * k + n, partner) for n in range(4)]
        )
    b1, b2 = seq_of(rows[1], x, core), seq_of(rows[2], x, core)
    up_own = remote(kvb.at[seq], kvb.at[seq], sems, 30, up)
    in_own = remote(kvb.at[seq], kvb.at[b1], sems, 30, up)
    up_next = remote(kvb.at[b1], kvb.at[b1], sems, 31, up)
    in_next = remote(kvb.at[b1], kvb.at[b2], sems, 31, up)
    up_own.start()
    rings[0].start()
    across[0][0].start()
    column(3, o, 0)
    column(3, o, 1)
    for h in range(4):
        piece = acc[:, pl.ds(h * HEAD, HEAD)].astype(BF16)
        qs[heads[h], :] = piece
        qt[pl.ds(0, HEAD), heads[h]] = piece.astype(F32).T.astype(BF16)
    number = lax.broadcasted_iota(jnp.int32, (HEAD, TOK), 0).astype(F32)
    other = jnp.where(number == docs, 0.0, MASKED).astype(BF16)
    for h in range(4):
        qt[pl.ds(HEAD, HEAD), heads[h]] = other
    m_buf[...] = jnp.full(m_buf.shape, MASKED, F32)
    m_run[...] = jnp.full(m_run.shape, MASKED, F32)
    l_buf[...] = jnp.zeros(l_buf.shape, F32)
    o_acc[...] = jnp.zeros(o_acc.shape, F32)
    dq_acc[...] = jnp.zeros(dq_acc.shape, F32)

    def score(b, diagonal):
        key_docs = kvb[b, pl.ds(TOK, 16), :].astype(F32)[0:1, :]
        same = jnp.where(number == key_docs, 1.0, 0.0)
        ka[:, pl.ds(0, HEAD)] = kvb[b, whole, pl.ds(0, HEAD)]
        ka[:, pl.ds(HEAD, HEAD)] = same.T.astype(BF16)
        for h in range(4):
            s = jnp.dot(ka[...], qt[:, heads[h]], preferred_element_type=F32)
            if diagonal:
                key_at = lax.broadcasted_iota(jnp.int32, (TOK, TOK), 0)
                query_at = lax.broadcasted_iota(jnp.int32, (TOK, TOK), 1)
                s = jnp.where(key_at <= query_at, s, MASKED)
            s_buf[seq - b, :, heads[h]] = s
            m_buf[:, heads[h]] = jnp.maximum(m_buf[:, heads[h]], s.reshape(TOK // 8, 8, TOK).max(axis=0))

    def raise_top():
        top = jnp.maximum(jnp.max(m_buf[...], axis=0, keepdims=True), m_run[0:1, :])
        factor = jnp.exp2((m_run[0:1, :] - top) * (SCALE * LOG2E))
        m_run[...] = jnp.broadcast_to(top, m_run.shape)
        l_buf[...] = l_buf[...] * factor
        o_acc[...] = o_acc[...] * factor

    def mix(b):
        values = kvb[b, whole, pl.ds(HEAD, HEAD)]
        for h in range(4):
            s = s_buf[seq - b, :, heads[h]]
            p = jnp.exp2((s - m_run[0:1, heads[h]]) * (SCALE * LOG2E))
            l_buf[:, heads[h]] += p.reshape(TOK // 8, 8, TOK).sum(axis=0)
            o_acc[:, heads[h]] += lax.dot_general(
                values, p.astype(BF16), TN, preferred_element_type=F32
            )

    def sweep(step, lo, hi):
        def one(b, carry):
            step(b)
            return carry

        lax.fori_loop(lo, hi, one, 0)

    low1 = jnp.maximum(8 * y - 8, 0)
    low2 = jnp.maximum(seq - (BAND - 1), 0)
    score(seq, True)
    rings[0].forward()
    in_own.wait_recv()
    up_next.start()
    rings[1].start()
    across[1][0].start()
    rings[0].wait_left()
    across[0][1].start()
    rings[0].wait_right()
    across[0][2].start()
    in_next.wait_recv()
    rings[2].start()
    across[2][0].start()
    rings[0].wait_far()
    across[0][3].start()
    g_ring.forward()
    rings[1].forward()
    for copy in across_in[0]:
        copy.wait_recv()
    sweep(lambda b: score(b, False), 8 * y, seq)
    raise_top()
    rings[1].wait_left()
    across[1][1].start()
    rings[1].wait_right()
    across[1][2].start()
    rings[1].wait_far()
    across[1][3].start()
    rings[2].forward()
    sweep(mix, 8 * y, seq + 1)
    for copy in across_in[1]:
        copy.wait_recv()
    sweep(lambda b: score(b, False), low1, 8 * y)
    raise_top()
    rings[2].wait_left()
    across[2][1].start()
    rings[2].wait_right()
    across[2][2].start()
    rings[2].wait_far()
    across[2][3].start()
    sweep(mix, low1, 8 * y)
    g_ring.wait_left()
    fold_grad(1, l)
    for copy in across_in[2]:
        copy.wait_recv()
    sweep(lambda b: score(b, False), low2, low1)
    raise_top()
    sweep(mix, low2, low1)

    inverse = 1.0 / jnp.sum(l_buf[...], axis=0, keepdims=True)
    li_buf[...] = jnp.broadcast_to(inverse, (8, 1024))
    for h in range(4):
        mixed = o_acc[:, heads[h]] * inverse[:, h * TOK : (h + 1) * TOK]
        att[:, pl.ds(h * HEAD, HEAD)] = mixed.T.astype(BF16)
    g_ring.wait_right()
    fold_grad(2, r)
    g_ring.wait_far()
    fold_grad(3, o)
    g_ring.finish()
    for h in range(4):
        grad = go_acc[:, pl.ds(h * HEAD, HEAD)].astype(BF16)
        do_buf[heads[h], :] = grad
        grad = grad.astype(F32)
        dot_buf[:, heads[h]] = grad.T.astype(BF16)
        mixed = att[:, pl.ds(h * HEAD, HEAD)].astype(F32)
        d_buf[:, heads[h]] = jnp.broadcast_to(
            jnp.sum((grad * mixed).T, axis=0, keepdims=True), (8, TOK)
        )

    def branch_term(slot):
        g_buf[slot] = jnp.dot(att[...], w_out[slot], preferred_element_type=F32).astype(BF16)

    b_ring = RingReduce(
        lambda slot, part: g_buf.at[slot, part], brelay, bfinal, slots, HALF, TOK, zsems, 15, zright, zleft
    )
    branch_term(o)
    b_ring.start_far()
    branch_term(r)
    branch_term(l)
    b_ring.start_near()

    def back(b, k):
        keys = kvb[b, whole, pl.ds(0, HEAD)]
        values = kvb[b, whole, pl.ds(HEAD, HEAD)]
        key_grad = jnp.zeros((TOK, HEAD), F32)
        value_grad = jnp.zeros((TOK, HEAD), F32)
        for h in range(4):
            s = s_buf[seq - b, :, heads[h]]
            p = jnp.exp2((s - m_run[0:1, heads[h]]) * (SCALE * LOG2E)) * li_buf[0:1, heads[h]]
            dp = jnp.dot(values, dot_buf[:, heads[h]], preferred_element_type=F32)
            ds = (p * (dp - d_buf[0:1, heads[h]])).astype(BF16)
            value_grad += jnp.dot(p.astype(BF16), do_buf[heads[h], :], preferred_element_type=F32)
            key_grad += jnp.dot(ds, qs[heads[h], :], preferred_element_type=F32)
            dq_acc[:, heads[h]] += lax.dot_general(keys, ds, TN, preferred_element_type=F32)
        i = b - 8 * (y - k)
        to = dkv.at[k, lax.div(i, 2), lax.rem(i, 2)]
        to[:, pl.ds(0, HEAD)] = (key_grad * SCALE).astype(BF16)
        to[:, pl.ds(HEAD, HEAD)] = value_grad.astype(BF16)

    over = [remote(dkv.at[k, :, 1 - core], twin.at[k], sems, 32 + k, partner) for k in range(3)]
    sum_rings = [
        RingReduce(
            lambda slot, part, k=k: sums.at[k, slot, part],
            xrelay.at[k], xfinal.at[k], (x, xl, xr, xo), HALF, TOK, sems, 35 + 6 * k, right, left,
        )
        for k in range(3)
    ]

    def open_ring(k):
        over[k].wait_recv()

        def add(i, carry):
            sums[k, i] = (dkv[k, i, core].astype(F32) + twin[k, i].astype(F32)).astype(BF16)
            return carry

        lax.fori_loop(0, 4, add, 0)
        sum_rings[k].start_far()
        sum_rings[k].start_near()

    far_up = remote(yown.at[0], ynear.at[0], sems, 53, down)
    near_up = remote(yown.at[1], ynear.at[1], sems, 54, down)
    mid1 = jnp.maximum(8 * y - 4, 0)
    mid0 = jnp.minimum(8 * y + 4, seq)
    sweep(lambda b: back(b, 2), low2, low1)
    over[2].start()
    sweep(lambda b: back(b, 1), low1, mid1)
    open_ring(2)
    b_ring.forward()
    sweep(lambda b: back(b, 1), mid1, 8 * y)
    over[1].start()
    sum_rings[2].forward()
    sweep(lambda b: back(b, 0), 8 * y, mid0)
    open_ring(1)
    yown[0] = sum_rings[2].wait_total()(whole).astype(BF16)
    far_up.start()
    sweep(lambda b: back(b, 0), mid0, seq + 1)
    over[0].start()
    sum_rings[1].forward()
    branch_term(me)
    grads_q = dq_acc[...] * SCALE
    for h in range(4):
        grads[:, pl.ds(h * HEAD, HEAD)] = grads_q[:, h * TOK : (h + 1) * TOK].T.astype(BF16)
    open_ring(0)
    total = sum_rings[1].wait_total()(whole)
    far_up.wait_recv()
    yown[1] = (total + ynear[0].astype(F32)).astype(BF16)
    near_up.start()
    sum_rings[0].forward()
    dots = jnp.zeros((TOK, 1), F32)
    for h in range(4):
        dots += jnp.sum(
            qs[heads[h], :].astype(F32) * grads[:, pl.ds(h * HEAD, HEAD)].astype(F32), axis=-1, keepdims=True
        )
    total = b_ring.wait_total()
    for part in (pl.ds(0, HALF), pl.ds(HALF, HALF)):
        branch_ref[part, :] = total(part)
    total = sum_rings[0].wait_total()(whole)
    near_up.wait_recv()
    grads[:, pl.ds(512, 256)] = (total + ynear[1].astype(F32)).astype(BF16)

    def norm_term(slot):
        for i in range(4):
            at = pl.ds(pl.multiple_of(slot * COLS + i * 256, 256), 256)
            piece = lax.dot_general(grads[...], weights[at, :], NT, preferred_element_type=F32)
            x_buf[slot, :, pl.ds(i * 256, 256)] = piece.astype(BF16)

    x_ring.finish()
    n_ring = RingReduce(
        lambda slot, part: x_buf.at[slot, part], nrelay, nfinal, slots, HALF, TOK, zsems, 21, zright, zleft
    )
    norm_term(o)
    n_ring.start_far()
    norm_term(r)
    norm_term(l)
    n_ring.start_near()
    dots += jnp.sum(
        kvb[seq, whole, :].astype(F32) * grads[:, pl.ds(512, 256)].astype(F32), axis=-1, keepdims=True
    )
    mine[1] = jnp.broadcast_to(dots, (TOK, 128)).T[0:8, :]
    small_dots = exchange(1, 27)
    for copy in small_dots:
        copy.start()
    norm_term(me)
    n_ring.forward()
    for copy in small_dots:
        copy.wait_recv()
    dot_ref[...] = mine[1] + theirs[1, 0] + theirs[1, 1] + theirs[1, 2]
    total = n_ring.wait_total()
    for part in (pl.ds(0, HALF), pl.ds(HALF, HALF)):
        out_ref[part, :] = total(part)
    for copy in small + small_dots + over + [far_up, near_up, up_own, up_next]:
        copy.wait_send()
    for ring in rings + sum_rings + [b_ring, n_ring]:
        ring.finish()
    for k in range(3):
        for n in range(4):
            across[k][n].wait_send()


def block(x, g, docs, gain, w_query, w_key, w_value, w_out):
    return pl.pallas_call(
        block_kernel,
        name="block",
        out_shape=(
            jax.ShapeDtypeStruct((TOK, COLS), F32),
            jax.ShapeDtypeStruct((TOK, COLS), F32),
            jax.ShapeDtypeStruct((8, TOK), F32),
            jax.ShapeDtypeStruct((TOK, 128), F32),
        ),
        in_specs=[ANY, ANY, VM, VM, ANY, ANY, ANY, ANY],
        out_specs=(VM, VM, VM, VM),
        scratch_shapes=[
            pltpu.VMEM((4, TOK, COLS), BF16),
            pltpu.VMEM((4, TOK, COLS), BF16),
            pltpu.VMEM((WIDTH, 768), BF16),
            pltpu.VMEM((4, 512, COLS), BF16),
            pltpu.VMEM((TOK, 768), F32),
            pltpu.VMEM((TOK, 512), F32),
            pltpu.VMEM((TOK, COLS), BF16),
            pltpu.VMEM((2, 8, TOK), F32),
            pltpu.VMEM((2, 3, 8, TOK), F32),
            pltpu.VMEM((32, ROWS_KV, 256), BF16),
            pltpu.VMEM((BAND, TOK, 1024), F32),
            pltpu.VMEM((TOK, 256), BF16),
            pltpu.VMEM((256, 1024), BF16),
            pltpu.VMEM((1024, HEAD), BF16),
            pltpu.VMEM((HEAD, 1024), BF16),
            pltpu.VMEM((1024, HEAD), BF16),
            pltpu.VMEM((HEAD, 1024), F32),
            pltpu.VMEM((HEAD, 1024), F32),
            pltpu.VMEM((8, 1024), F32),
            pltpu.VMEM((8, 1024), F32),
            pltpu.VMEM((8, 1024), F32),
            pltpu.VMEM((8, 1024), F32),
            pltpu.VMEM((8, 1024), F32),
            pltpu.VMEM((TOK, 512), BF16),
            pltpu.VMEM((3, 4, 2, TOK, 256), BF16),
            pltpu.VMEM((3, 4, TOK, 256), BF16),
            pltpu.VMEM((3, 4, TOK, 256), BF16),
            pltpu.VMEM((3, 2, HALF, 256), BF16),
            pltpu.VMEM((3, 2, TOK, 256), BF16),
            pltpu.VMEM((2, TOK, 256), BF16),
            pltpu.VMEM((2, TOK, 256), BF16),
            pltpu.VMEM((2, HALF, COLS), BF16),
            pltpu.VMEM((2, TOK, COLS), BF16),
            pltpu.VMEM((2, HALF, COLS), BF16),
            pltpu.VMEM((2, TOK, COLS), BF16),
            pltpu.VMEM((TOK, 768), BF16),
            DMA((18,)),
            DMA((30,)),
            DMA((30,)),
            DMA((55,)),
            DMA((55,)),
        ],
        compiler_params=pltpu.CompilerParams(
            collective_id=0, has_side_effects=True, vmem_limit_bytes=63 * MIB
        ),
    )(x, g, docs, gain, w_query, w_key, w_value, w_out)


def per_device(
    y_first, x_second, grad_first, grad_second, doc_ids, norm_gain, w_query, w_key, w_value, w_out
):
    mp = lax.axis_index("mp")
    branch, shared, dots, inverse = block(
        x_second, grad_first, doc_ids.reshape(1, TOK), norm_gain.reshape(1, WIDTH),
        w_query, w_key, w_value, w_out,
    )
    x_first = y_first.astype(F32) - branch
    inverse = inverse[:, :1]
    unit = x_second.astype(F32) * inverse
    gain = lax.dynamic_slice_in_dim(norm_gain, mp * COLS, COLS, 0)
    mean = (dots[0] * (1.0 / WIDTH))[:, None]
    x_grad = grad_second.astype(F32) + inverse * (shared * gain - unit * mean)
    return (x_first, x_grad)


def solution(mesh):
    placed = (
        P("seq", "mp"),
        P("seq", "mp"),
        P("seq", "mp"),
        P("seq", "mp"),
        P("seq"),
        P(),
        P(None, "mp"),
        P(None, "mp"),
        P(None, "mp"),
        P("mp", None),
    )
    return jax.shard_map(
        per_device,
        mesh=mesh,
        in_specs=placed,
        out_specs=(P("seq", "mp"), P("seq", "mp")),
        check_vma=False,
    )
```

time: 762 us -> 119 us (0.16)
  waiting for transfers between devices: 311 us -> 0 us
  local copies, waits for them, and re-layouts: 224 us -> 1.7 us
  loops' own time: 121 us -> 0 us
  Pallas kernels: 0 us -> 112 us
  matrix products: 33.9 us -> 0 us
  other arithmetic: 32.3 us -> 4.18 us
  starting transfers between devices: 21 us -> 0 us
  between operations: 14.1 us -> 0.65 us
    reduce_scatter x1 -> x0, waiting for transfers between devices: 187 us -> none  [side_by_side_2(): lax.psum_scatter(both, axis, scatter_dimension=dim, tiled=True)]
    another operation x66 -> x0, loops' own time: 121 us -> none  [the longest x1 65.1 us: per_device(): running = lax.fori_loop(0, cycle_size, fold_forward, start_state)]
    pallas_call x0 -> x1, Pallas kernels: none -> 112 us  [block(): pl.pallas_call(block_kernel, name='block', out_shape=(jax.ShapeDtypeStruc...]
    slice x193 -> x1, local copies, waits for them, and re-layouts: 113 us -> 1.01 us  [per_device(): inverse = inverse[:, :1]]
    all_gather x2 -> x0, waiting for transfers between devices: 80.6 us -> none  [side_by_side(): whole, at, done = (lax.all_gather(both, axis, axis=dim, tiled=True), 0, [])]
    dynamic_slice x129 -> x1, local copies, waits for them, and re-layouts: 63.7 us -> 0.69 us  [per_device(): gain = lax.dynamic_slice_in_dim(norm_gain, mp * COLS, COLS, 0)]
    all_to_all x4 -> x0, waiting for transfers between devices: 42.4 us -> none  [the longest x2 39.6 us: sum_at_owner(): tiles = lax.all_to_all(cut_along(value, dim, size), axis, 0, 0, tiled=True)]
    dot_general x22 -> x0, matrix products: 33.9 us -> none  [the longest x1 5.44 us: per_device(): jnp.dot(attended.reshape(tok_rows, -1), w_out, preferred_element_type=jnp...]
  transfers between devices with their start and end apart: 7 -> 0, of which waited for: 5 -> 0; matrix products, arithmetic and copies ran while one was open for 7% -> 0% of each run, Pallas kernels for 0% -> 0%
where the time goes in v2:
time: 119 us
  Pallas kernels  112 us (94%)
  other arithmetic  4.18 us (4%)
  local copies, waits for them, and re-layouts  1.7 us (1%)
    pallas_call x1, Pallas kernels, block(): pl.pallas_call(block_kernel, name='block', out_shape=(jax.ShapeDtypeStruc...  112 us
    add x1, other arithmetic, per_device(): x_grad = grad_second.astype(F32) + inverse * (shared * gain - unit * mean)  3.47 us

profile of v2, /device:TPU:30, one launch (start us, length us, event | category | flops | bytes accessed | tf_op | source)
XLA Modules:
  0.0 119.0 jit_solution(521551742877451708)
XLA Ops:
  0.6 0.7 dynamic_slice.3
  1.3 0.0 copy-start
  1.3 112.5 %block.1 = (f32[256,1024]{1,0:T(8,128)}, f32[256,1024]{1,0:T(8,128)}, f32[8,256]{1,0:T(8,128)}, f32[256,128]{1,0:T(8,128)}) custom-call(bf16[256,1024]{1,0:T(8,128)(2,1)} %x_ref.1, bf16[256,1024]{1,0:T(8,128)(2,1)} %g_ref.1, s32[1,256]{1,0:T(1,128)} %bitcast.5, f32[1,4096]{1,0:T(1,128)} %bitcast.3, bf16[4096,512]{1,0:T(8,128)(2,1)} %wq_ref.1, ...), custom_call_target="tpu_custom_call" | custom-call | tf_op jit(solution)/shard_map/block/pallas_call | solution.py:549
  113.8 1.0 slice_reduce_fusion
  114.8 0.7 slice_multiply_fusion
  115.5 0.0 copy-done
  115.5 3.5 %multiply_add_fusion = (f32[256,1024]{1,0:T(8,128)}, f32[256,1024]{1,0:T(8,128)}) fusion(bf16[256,1024]{1,0:T(8,128)(2,1)S(1)} %copy-done, f32[256,1024]{1,0:T(8,128)} %get-tuple-element.8, bf16[256,1024]{1,0:T(8,128)(2,1)} %param.13, f32[256]{0:T(256)S(1)} %bitcast.4, f32[1024]{0:T(1024)S(1)} %dynamic_slice.3, f32[256]{0:T(256)S(1)} %slice_reduce_fusion, ...), kind=kLoop, calls=%fused_computation | loop fusion | flops 2621440 | bytes 5773312 | tf_op jit(solution)/shard_map/add | solution.py:622
Async XLA Ops:
  1.3 114.2 %copy-start = (bf16[256,1024]{1,0:T(8,128)(2,1)S(1)}, bf16[256,1024]{1,0:T(8,128)(2,1)}, u32[]{:S(2)}) copy-start(bf16[256,1024]{1,0:T(8,128)(2,1)} %x_ref.1) | copy-start | bytes 1572868

commit v3 on v2

v3 whole, which is shorter than its diff:
```python
import jax
import jax.numpy as jnp
from jax import lax
from jax.experimental import pallas as pl
from jax.experimental.pallas import tpu as pltpu
from jax.sharding import PartitionSpec as P

HEAD = 128
EPSILON = 1e-05
MASKED = -1e30
SCALE = HEAD**-0.5
LOG2E = 1.4426950408889634
TOK = 256
HALF = TOK // 2
COLS = 1024
WIDTH = 4096
BAND = 17
ROWS_KV = TOK + 16
MIB = 1 << 20
NT = (((1,), (1,)), ((), ()))
TN = (((0,), (0,)), ((), ()))
F32 = jnp.float32
BF16 = jnp.bfloat16


def place():
    seq, mp = lax.axis_index("seq"), lax.axis_index("mp")
    core = lax.rem(seq, 2)
    x = lax.rem(lax.div(seq, 2), 4)
    y = lax.div(seq, 8)
    return seq, mp, y, x, core


def seq_of(y, x, core):
    return y * 8 + x * 2 + core


def plus(a, b, n=4):
    return lax.rem(a + (b + n) % n, n)


def remote(src, dst, sems, index, device):
    send, recv = sems
    return pltpu.make_async_remote_copy(
        src_ref=src,
        dst_ref=dst,
        send_sem=send.at[index],
        recv_sem=recv.at[index],
        device_id=device,
        device_id_type=pl.DeviceIdType.MESH,
    )


def greet(devices):
    barrier = pltpu.get_barrier_semaphore()
    for device in devices:
        pl.semaphore_signal(barrier, inc=1, device_id=device, device_id_type=pl.DeviceIdType.MESH)
    return lambda: pl.semaphore_wait(barrier, len(devices))


class RingGather:
    def __init__(self, own, buf, slots, first, half, rows, sems, base, right, left, at=None):
        me, l, r, o = slots
        a, b = pl.ds(first, half), pl.ds(first + half, rows - half)
        at = at or (lambda slot, part: buf.at[slot, part])
        take = (lambda part: own.at[part]) if own is not None else (lambda part: at(me, part))
        mk = lambda src, dst, i, dev: remote(src, dst, sems, base + i, dev)
        self.out = [
            mk(take(a), at(me, a), 0, right),
            mk(take(b), at(me, b), 1, right),
            mk(take(b), at(me, b), 2, left),
            mk(take(a), at(me, a), 3, left),
            mk(at(l, a), at(l, a), 4, right),
            mk(at(r, b), at(r, b), 5, left),
        ]
        self.inn = [
            mk(take(a), at(l, a), 0, right),
            mk(take(b), at(l, b), 1, right),
            mk(take(b), at(r, b), 2, left),
            mk(take(a), at(r, a), 3, left),
            mk(take(a), at(o, a), 4, right),
            mk(take(b), at(o, b), 5, left),
        ]

    def start_first(self):
        self.out[0].start()
        self.out[2].start()

    def start_second(self):
        self.out[1].start()
        self.out[3].start()

    def start(self):
        self.start_first()
        self.start_second()

    def forward(self):
        self.inn[0].wait_recv()
        self.out[4].start()
        self.inn[2].wait_recv()
        self.out[5].start()

    def wait_left(self):
        self.inn[1].wait_recv()

    def wait_right(self):
        self.inn[3].wait_recv()

    def wait_far(self):
        self.inn[4].wait_recv()
        self.inn[5].wait_recv()

    def finish(self):
        for copy in self.out:
            copy.wait_send()


class RingReduce:
    def __init__(self, parts, relay, finals, slots, half, rows, sems, base, right, left):
        me, l, r, o = slots
        a, b = pl.ds(0, half), pl.ds(half, rows - half)
        self.parts, self.relay, self.finals = parts, relay, finals
        self.slots, self.a, self.b = slots, a, b
        mk = lambda src, dst, i, dev: remote(src, dst, sems, base + i, dev)
        self.out = [
            mk(parts(o, a), relay.at[0], 0, right),
            mk(parts(o, b), relay.at[1], 1, left),
            mk(parts(r, b), finals.at[0, b], 2, right),
            mk(parts(l, a), finals.at[1, a], 3, left),
            mk(parts(r, a), finals.at[0, a], 4, right),
            mk(parts(l, b), finals.at[1, b], 5, left),
        ]

    def start_far(self):
        self.out[0].start()
        self.out[1].start()

    def start_near(self):
        self.out[2].start()
        self.out[3].start()

    def forward(self):
        me, l, r, o = self.slots
        for i, slot, part in ((0, r, self.a), (1, l, self.b)):
            self.out[i].wait_recv()
            piece = self.parts(slot, part)
            piece[...] = (piece[...].astype(F32) + self.relay[i].astype(F32)).astype(BF16)
            self.out[4 + i].start()

    def wait_total(self):
        for i in (2, 3, 4, 5):
            self.out[i].wait_recv()
        me = self.slots[0]
        return lambda part: (
            self.parts(me, part)[...].astype(F32)
            + self.finals[0, part].astype(F32)
            + self.finals[1, part].astype(F32)
        )

    def finish(self):
        for copy in self.out:
            copy.wait_send()


def z_places(seq, mp):
    right, left, far = plus(mp, 1), plus(mp, -1), plus(mp, 2)
    return (mp, left, right, far), (seq, right), (seq, left), (seq, far)


VM = pl.BlockSpec(memory_space=pltpu.VMEM)
ANY = pl.BlockSpec(memory_space=pl.ANY)
DMA = pltpu.SemaphoreType.DMA


def block_kernel(x_ref, g_ref, y_ref, g2_ref, docs_ref, gain_ref, wq_ref, wk_ref, wv_ref, wo_ref,
                 first_ref, grad_ref, inv_ref, x_own, y_own, g2_own, p_buf, ds_buf, wkv, kv_all,
                 x_buf, g_buf, weights, w_out, acc, go_acc, scaled, mine, theirs, kvb, s_buf, ka, qt, qs,
                 dot_buf, o_acc, dq_acc, m_buf, m_run, t_buf, l_buf, d_buf, att, dkv, twin, sums,
                 xrelay, xfinal, ynear, yown, brelay, bfinal, nrelay, nfinal, grads,
                 lsem, zsend, zrecv, send, recv):
    seq, mp, y, x, core = place()
    slots, zright, zleft, zfar = z_places(seq, mp)
    me, l, r, o = slots
    zsems, sems = (zsend, zrecv), (send, recv)
    xr, xl, xo = plus(x, 1), plus(x, -1), plus(x, 2)
    up, down = (seq_of(plus(y, 1), x, core), mp), (seq_of(plus(y, -1), x, core), mp)
    right, left = (seq_of(y, xr, core), mp), (seq_of(y, xl, core), mp)
    partner = (seq_of(y, x, 1 - core), mp)
    above = (seq_of(plus(y, 2), x, core), mp)
    yu, yd, yo = plus(y, 1), plus(y, -1), plus(y, 2)
    rows = [plus(y, -k) for k in range(3)]
    heads = [pl.ds(h * TOK, TOK) for h in range(4)]
    whole = pl.ds(0, TOK)

    met = greet([up, down, above, right, left, partner, zright, zleft, zfar])

    x_load = pltpu.make_async_copy(x_ref, x_buf.at[me], lsem.at[0])
    x_load.start()
    loads = []
    for n, slot in enumerate((me, l, r, o)):
        at = pl.ds(pl.multiple_of(slot * COLS, COLS), COLS)
        group = []
        for i, (w, lo, hi) in enumerate(((wq_ref, 0, 512), (wk_ref, 512, 640), (wv_ref, 640, 768))):
            copy = pltpu.make_async_copy(w.at[at], weights.at[at, pl.ds(lo, hi - lo)], lsem.at[1 + 3 * n + i])
            copy.start()
            group.append(copy)
        loads.append(group)
    g_load = pltpu.make_async_copy(g_ref, g_buf.at[me], lsem.at[13])
    g_load.start()
    w_loads = []
    for n, slot in enumerate((me, l, r, o)):
        cols = pl.ds(pl.multiple_of(slot * COLS, COLS), COLS)
        copy = pltpu.make_async_copy(wo_ref.at[:, cols], w_out.at[slot], lsem.at[14 + n])
        copy.start()
        w_loads.append(copy)
    late = []
    for i, (src, dst) in enumerate(((x_ref, x_own), (y_ref, y_own), (g2_ref, g2_own))):
        copy = pltpu.make_async_copy(src, dst, lsem.at[18 + i])
        copy.start()
        late.append(copy)

    x_rings = [
        RingGather(x_ref, x_buf, slots, i * HALF, HALF // 2, HALF, zsems, 30 * i, zright, zleft) for i in range(2)
    ]
    met()
    x_rings[0].start_first()
    x_load.wait()
    values = x_buf[me].astype(F32)
    squares = jnp.sum(values * values, axis=-1, keepdims=True)
    mine[0] = jnp.broadcast_to(squares, (TOK, 128)).T[0:8, :]

    def exchange(which, base):
        return [
            remote(mine.at[which], theirs.at[which, i], zsems, base + i, device)
            for i, device in enumerate((zright, zleft, zfar))
        ]

    small = exchange(0, 6)
    for copy in small:
        copy.start()
    x_rings[0].start_second()
    docs = docs_ref[...].astype(F32)
    kvb[seq, pl.ds(TOK, 16), :] = jnp.broadcast_to(docs, (16, TOK)).astype(BF16)

    def clear(i, carry):
        for k in range(3):
            for c in range(2):
                dkv[k, i, c] = jnp.zeros((TOK, 256), BF16)
        return carry

    lax.fori_loop(0, 4, clear, 0)
    for copy in small:
        copy.wait_recv()
    squares = mine[0] + theirs[0, 0] + theirs[0, 1] + theirs[0, 2]
    inverse = lax.rsqrt(squares[0:1, :] * (1.0 / WIDTH) + EPSILON)
    inv_ref[...] = jnp.broadcast_to(inverse, (128, TOK)).T

    def column(n, slot, i, part):
        at = pl.ds(pl.multiple_of(slot * COLS, COLS), COLS)
        cols = pl.ds(i * 256, 256)
        term = jnp.dot(scaled[part, :], weights[at, cols], preferred_element_type=F32)
        acc[part, cols] = term if n == 0 else acc[part, cols] + term

    def scale_rows(slot, part):
        gain = gain_ref[:, pl.ds(pl.multiple_of(slot * COLS, COLS), COLS)]
        scaled[part, :] = (x_buf[slot, part, :].astype(F32) * inv_ref[part, 0:1] * gain).astype(BF16)

    def fold(n, slot, part):
        scale_rows(slot, part)
        for i in range(3):
            column(n, slot, i, part)

    def fold_grad(n, slot):
        w_loads[n].wait()
        term = lax.dot_general(g_buf[slot], w_out[slot], NT, preferred_element_type=F32)
        go_acc[...] = term if n == 0 else go_acc[...] + term

    halves = (pl.ds(0, HALF), pl.ds(HALF, HALF))
    sent = (pl.ds(0, HALF), pl.ds(HALF, ROWS_KV - HALF))
    rings, across, across_in = [], [], []
    for k in range(3):
        at = [seq_of(rows[k], column_, core) for column_ in (x, xl, xr, xo)]
        there = [seq_of(rows[k], column_, 1 - core) for column_ in (x, xl, xr, xo)]
        rings.append([
            RingGather(
                kvb.at[at[0]], kvb, at, i * HALF, 64, (HALF, ROWS_KV - HALF)[i], sems, 12 * k + 6 * i, right, left
            )
            for i in range(2)
        ])
        across.append([
            [remote(kvb.at[at[n], sent[i]], kvb.at[at[n], sent[i]], sems, 36 + 8 * k + 2 * n + i, partner)
             for n in range(4)] for i in range(2)
        ])
        across_in.append([
            [remote(kvb.at[at[n], sent[i]], kvb.at[there[n], sent[i]], sems, 36 + 8 * k + 2 * n + i, partner)
             for n in range(4)] for i in range(2)
        ])
    b1, b2 = seq_of(rows[1], x, core), seq_of(rows[2], x, core)

    def lift(dst, base, device):
        return [remote(kvb.at[seq, sent[i]], kvb.at[dst, sent[i]], sems, base + i, device) for i in range(2)]

    up_own, in_own = lift(seq, 60, up), lift(b1, 60, up)
    up_next, in_next = lift(seq, 62, above), lift(b2, 62, above)

    def launch(i):
        kvb[seq, halves[i], :] = acc[halves[i], pl.ds(512, 256)].astype(BF16)
        up_own[i].start()
        up_next[i].start()
        rings[0][i].start()
        across[0][i][0].start()

    def second_row(i):
        in_own[i].wait_recv()
        rings[1][i].start()
        across[1][i][0].start()

    def third_row(i):
        in_next[i].wait_recv()
        rings[2][i].start()
        across[2][i][0].start()

    def near(k, i):
        rings[k][i].wait_left()
        across[k][i][1].start()
        rings[k][i].wait_right()
        across[k][i][2].start()

    def pass_on(k, i):
        near(k, i)
        rings[k][i].wait_far()
        across[k][i][3].start()

    g_ring = RingGather(g_ref, g_buf, slots, 0, HALF, TOK, zsems, 9, zright, zleft)
    for group in loads:
        for copy in group:
            copy.wait()
    slot = 2 * x + core
    pieces = []
    for i, (target, device) in enumerate(((r, zright), (l, zleft), (o, zfar))):
        at = pl.ds(pl.multiple_of(target * COLS + seq * 32, 32), 32)
        pieces.append(remote(weights.at[at, pl.ds(512, 256)], wkv.at[i, y, slot], zsems, 36 + i, device))
    y_pieces = RingGather(
        None, None, (y, yd, yu, yo), 0, 16, 32, sems, 87, up, down,
        at=lambda row, part: wkv.at[:, row, slot, part],
    )
    x_pieces = RingGather(
        None, None, (x, xl, xr, xo), 0, 16, 32, sems, 93, right, left,
        at=lambda column_, part: wkv.at[:, :, 2 * column_ + core, part],
    )
    over_pieces = [
        remote(wkv.at[:, :, 2 * n + core], wkv.at[:, :, 2 * n + core], sems, 99 + n, partner) for n in range(4)
    ]
    over_in = [
        remote(wkv.at[:, :, 2 * n + core], wkv.at[:, :, 2 * n + 1 - core], sems, 99 + n, partner) for n in range(4)
    ]
    x_rings[0].forward()
    for copy in pieces:
        copy.start()
    x_rings[1].start()
    fold(0, me, whole)
    x_rings[0].wait_left()
    fold(1, l, halves[0])
    x_rings[0].wait_right()
    fold(2, r, halves[0])
    x_rings[0].wait_far()
    scale_rows(o, halves[0])
    column(3, o, 2, halves[0])
    launch(0)
    x_rings[1].forward()
    g_ring.start()
    column(3, o, 0, halves[0])
    column(3, o, 1, halves[0])
    rings[0][0].forward()
    second_row(0)
    third_row(0)
    x_rings[1].wait_left()
    fold(1, l, halves[1])
    x_rings[1].wait_right()
    fold(2, r, halves[1])
    pass_on(0, 0)
    rings[1][0].forward()
    x_rings[1].wait_far()
    scale_rows(o, halves[1])
    column(3, o, 2, halves[1])
    launch(1)
    for copy in pieces:
        copy.wait_recv()
    y_pieces.start()
    rings[2][0].forward()
    column(3, o, 0, halves[1])
    column(3, o, 1, halves[1])
    pass_on(1, 0)
    for h in range(4):
        piece = acc[:, pl.ds(h * HEAD, HEAD)].astype(BF16)
        qs[heads[h], :] = piece
        qt[pl.ds(0, HEAD), heads[h]] = piece.astype(F32).T.astype(BF16)
    number = lax.broadcasted_iota(jnp.int32, (HEAD, TOK), 0).astype(F32)
    other = jnp.where(number == docs, 0.0, MASKED).astype(BF16)
    for h in range(4):
        qt[pl.ds(HEAD, HEAD), heads[h]] = other
    m_buf[...] = jnp.full(m_buf.shape, MASKED, F32)
    m_run[...] = jnp.full(m_run.shape, MASKED, F32)
    l_buf[...] = jnp.zeros(l_buf.shape, F32)
    o_acc[...] = jnp.zeros(o_acc.shape, F32)
    dq_acc[...] = jnp.zeros(dq_acc.shape, F32)

    def score(b, diagonal):
        key_docs = kvb[b, pl.ds(TOK, 16), :].astype(F32)[0:1, :]
        same = jnp.where(number == key_docs, 1.0, 0.0)
        ka[:, pl.ds(0, HEAD)] = kvb[b, whole, pl.ds(0, HEAD)]
        ka[:, pl.ds(HEAD, HEAD)] = same.T.astype(BF16)
        for h in range(4):
            s = jnp.dot(ka[...], qt[:, heads[h]], preferred_element_type=F32)
            if diagonal:
                key_at = lax.broadcasted_iota(jnp.int32, (TOK, TOK), 0)
                query_at = lax.broadcasted_iota(jnp.int32, (TOK, TOK), 1)
                s = jnp.where(key_at <= query_at, s, MASKED)
            s_buf[seq - b, :, heads[h]] = s
            m_buf[:, heads[h]] = jnp.maximum(m_buf[:, heads[h]], s.reshape(TOK // 8, 8, TOK).max(axis=0))

    def raise_top():
        top = jnp.maximum(jnp.max(m_buf[...], axis=0, keepdims=True), m_run[0:1, :])
        factor = jnp.exp2((m_run[0:1, :] - top) * (SCALE * LOG2E))
        m_run[...] = jnp.broadcast_to(top, m_run.shape)
        t_buf[...] = m_run[...] * (SCALE * LOG2E)
        l_buf[...] = l_buf[...] * factor
        o_acc[...] = o_acc[...] * factor

    def mix(b):
        values = kvb[b, whole, pl.ds(HEAD, HEAD)]
        for h in range(4):
            s = s_buf[seq - b, :, heads[h]]
            p = jnp.exp2(s * (SCALE * LOG2E) - t_buf[0:1, heads[h]])
            l_buf[:, heads[h]] += p.reshape(TOK // 8, 8, TOK).sum(axis=0)
            o_acc[:, heads[h]] += lax.dot_general(
                values, p.astype(BF16), TN, preferred_element_type=F32
            )

    def sweep(step, lo, hi):
        def one(b, carry):
            step(b)
            return carry

        lax.fori_loop(lo, hi, one, 0)

    def fold_grad_own():
        g_load.wait()
        fold_grad(0, me)

    low1 = jnp.maximum(8 * y - 8, 0)
    mid1 = jnp.maximum(8 * y - 4, 0)
    mid0 = jnp.minimum(8 * y + 4, seq)
    low2 = jnp.maximum(seq - (BAND - 1), 0)
    rings[0][1].forward()
    second_row(1)
    third_row(1)
    score(seq, True)
    pass_on(2, 0)
    pass_on(0, 1)
    y_pieces.forward()
    rings[1][1].forward()
    rings[2][1].forward()
    for copies in across_in[0]:
        for copy in copies:
            copy.wait_recv()
    sweep(lambda b: score(b, False), 8 * y, mid0)
    g_ring.forward()
    sweep(lambda b: score(b, False), mid0, seq)
    raise_top()
    pass_on(1, 1)
    sweep(mix, 8 * y, mid0)
    pass_on(2, 1)
    sweep(mix, mid0, seq + 1)
    y_pieces.wait_left()
    y_pieces.wait_right()
    y_pieces.wait_far()
    x_pieces.start()
    fold_grad_own()
    for copies in across_in[1]:
        for copy in copies:
            copy.wait_recv()
    sweep(lambda b: score(b, False), low1, 8 * y)
    raise_top()
    sweep(mix, low1, 8 * y)
    g_ring.wait_left()
    fold_grad(1, l)
    g_ring.wait_right()
    fold_grad(2, r)
    for copies in across_in[2]:
        for copy in copies:
            copy.wait_recv()
    sweep(lambda b: score(b, False), low2, low1)
    raise_top()
    sweep(mix, low2, low1)
    x_pieces.forward()
    g_ring.wait_far()
    fold_grad(3, o)
    for h in range(4):
        grad = go_acc[:, pl.ds(h * HEAD, HEAD)].astype(BF16)
        dot_buf[:, heads[h]] = grad.astype(F32).T.astype(BF16)
    g_ring.finish()

    total = jnp.sum(l_buf[...], axis=0, keepdims=True)
    inverse = 1.0 / total
    t_buf[...] = t_buf[...] + jnp.log2(total)
    for h in range(4):
        mixed = (o_acc[:, heads[h]] * inverse[:, h * TOK : (h + 1) * TOK]).astype(BF16).astype(F32)
        att[:, pl.ds(h * HEAD, HEAD)] = mixed.T.astype(BF16)
        delta = jnp.sum(dot_buf[:, heads[h]].astype(F32) * mixed, axis=0, keepdims=True)
        d_buf[:, heads[h]] = jnp.broadcast_to(delta, (8, TOK))

    def branch_term(slot):
        g_buf[slot] = jnp.dot(att[...], w_out[slot], preferred_element_type=F32).astype(BF16)

    b_ring = RingReduce(
        lambda slot, part: g_buf.at[slot, part], brelay, bfinal, slots, HALF, TOK, zsems, 15, zright, zleft
    )
    branch_term(o)
    b_ring.start_far()

    def back(b, k):
        keys = kvb[b, whole, pl.ds(0, HEAD)]
        values = kvb[b, whole, pl.ds(HEAD, HEAD)]
        for h in range(4):
            s = s_buf[seq - b, :, heads[h]]
            p = jnp.exp2(s * (SCALE * LOG2E) - t_buf[0:1, heads[h]])
            dp = jnp.dot(values, dot_buf[:, heads[h]], preferred_element_type=F32)
            p_buf[:, heads[h]] = p.astype(BF16)
            ds_buf[:, heads[h]] = (p * (dp - d_buf[0:1, heads[h]])).astype(BF16)
        dq_acc[...] += lax.dot_general(keys, ds_buf[...], TN, preferred_element_type=F32)
        value_grad = lax.dot_general(dot_buf[...], p_buf[...], NT, preferred_element_type=F32)
        key_grad = lax.dot_general(qt[pl.ds(0, HEAD), :], ds_buf[...], NT, preferred_element_type=F32)
        i = b - 8 * (y - k)
        to = dkv.at[k, lax.div(i, 2), lax.rem(i, 2)]
        to[pl.ds(0, HEAD), :] = (key_grad * SCALE).astype(BF16)
        to[pl.ds(HEAD, HEAD), :] = value_grad.astype(BF16)

    over = [remote(dkv.at[k, :, 1 - core], twin.at[k], sems, 64 + k, partner) for k in range(3)]
    sum_rings = [
        RingReduce(
            lambda slot, part, k=k: sums.at[k, slot, part],
            xrelay.at[k], xfinal.at[k], (x, xl, xr, xo), HALF, TOK, sems, 67 + 6 * k, right, left,
        )
        for k in range(3)
    ]

    def open_ring(k):
        over[k].wait_recv()

        def add(i, carry):
            sums[k, i] = (dkv[k, i, core].astype(F32) + twin[k, i].astype(F32)).astype(BF16)
            return carry

        lax.fori_loop(0, 4, add, 0)
        sum_rings[k].start_far()
        sum_rings[k].start_near()

    far_up = remote(yown.at[0], ynear.at[0], sems, 85, down)
    near_up = remote(yown.at[1], ynear.at[1], sems, 86, down)
    sweep(lambda b: back(b, 2), low2, low1)
    over[2].start()
    branch_term(r)
    branch_term(l)
    b_ring.start_near()
    sweep(lambda b: back(b, 1), low1, mid1)
    open_ring(2)
    b_ring.forward()
    sweep(lambda b: back(b, 1), mid1, 8 * y)
    over[1].start()
    x_pieces.wait_left()
    x_pieces.wait_right()
    x_pieces.wait_far()
    for copy in over_pieces:
        copy.start()
    sum_rings[2].forward()
    sweep(lambda b: back(b, 0), 8 * y, mid0)
    open_ring(1)
    yown[0] = sum_rings[2].wait_total()(whole).astype(BF16)
    far_up.start()
    sweep(lambda b: back(b, 0), mid0, seq + 1)
    over[0].start()
    grads_q = dq_acc[...] * SCALE
    for h in range(4):
        grads[:, pl.ds(h * HEAD, HEAD)] = grads_q[:, h * TOK : (h + 1) * TOK].T.astype(BF16)
    for ring in x_rings:
        ring.finish()

    def norm_term(slot):
        for i in range(4):
            at = pl.ds(pl.multiple_of(slot * COLS + i * 256, 256), 256)
            piece = lax.dot_general(
                grads[:, pl.ds(0, 512)], weights[at, pl.ds(0, 512)], NT, preferred_element_type=F32
            )
            x_buf[slot, :, pl.ds(i * 256, 256)] = piece.astype(BF16)

    n_ring = RingReduce(
        lambda slot, part: x_buf.at[slot, part], nrelay, nfinal, slots, HALF, TOK, zsems, 21, zright, zleft
    )
    norm_term(o)
    n_ring.start_far()
    sum_rings[1].forward()
    norm_term(r)
    norm_term(l)
    n_ring.start_near()
    open_ring(0)
    total = sum_rings[1].wait_total()(whole)
    far_up.wait_recv()
    yown[1] = (total + ynear[0].astype(F32)).astype(BF16)
    near_up.start()
    sum_rings[0].forward()
    branch_term(me)
    norm_term(me)
    dots = jnp.zeros((TOK, 1), F32)
    for h in range(4):
        dots += jnp.sum(
            qs[heads[h], :].astype(F32) * grads[:, pl.ds(h * HEAD, HEAD)].astype(F32), axis=-1, keepdims=True
        )
    for copy in late:
        copy.wait()
    total = b_ring.wait_total()
    for part in (pl.ds(0, HALF), pl.ds(HALF, HALF)):
        s_buf[0, part, :] = y_own[part, :].astype(F32) - total(part)
    first_out = pltpu.make_async_copy(s_buf.at[0], first_ref, lsem.at[21])
    first_out.start()
    n_ring.forward()
    total = sum_rings[0].wait_total()(whole)
    near_up.wait_recv()
    total = (total + ynear[1].astype(F32)).astype(BF16).astype(F32).T
    kv_all[me] = total.astype(BF16)
    kv_ring = RingGather(None, kv_all, slots, 0, HALF, TOK, zsems, 39, zright, zleft)
    kv_ring.start()
    dots += jnp.sum(kvb[seq, whole, :].astype(F32) * kv_all[me].astype(F32), axis=-1, keepdims=True)
    mine[1] = jnp.broadcast_to(dots, (TOK, 128)).T[0:8, :]
    small_dots = exchange(1, 27)
    for copy in small_dots:
        copy.start()

    for copy in over_in:
        copy.wait_recv()

    def kv_term(n, slot):
        for i in range(4):
            cols = pl.ds(i * 256, 256)
            if n == 0:
                at = pl.ds(pl.multiple_of(me * COLS + i * 256, 256), 256)
                w = weights[at, pl.ds(512, 256)]
            else:
                w = wkv[n - 1, i].reshape(256, 256)
            term = lax.dot_general(kv_all[slot], w, NT, preferred_element_type=F32)
            s_buf[2, :, cols] = term if n == 0 else s_buf[2, :, cols] + term

    kv_term(0, me)
    kv_ring.forward()
    kv_ring.wait_left()
    kv_term(1, l)
    kv_ring.wait_right()
    kv_term(2, r)
    for copy in small_dots:
        copy.wait_recv()
    mean = (mine[1] + theirs[1, 0] + theirs[1, 1] + theirs[1, 2])[0:1, :] * (1.0 / WIDTH)
    mean = jnp.broadcast_to(mean, (128, TOK)).T
    gain = gain_ref[:, pl.ds(pl.multiple_of(me * COLS, COLS), COLS)]
    total = n_ring.wait_total()
    kv_ring.wait_far()
    kv_term(3, o)
    grad_out = []
    for i in range(2):
        lo, hi, part = i * HALF, (i + 1) * HALF, pl.ds(i * HALF, HALF)
        inverse = inv_ref[part, 0:1]
        unit = x_own[part, :].astype(F32) * inverse
        s_buf[1, part, :] = g2_own[part, :].astype(F32) + inverse * (
            (total(part) + s_buf[2, part, :]) * gain - unit * mean[lo:hi, 0:1]
        )
        copy = pltpu.make_async_copy(s_buf.at[1, part], grad_ref.at[part], lsem.at[22 + i])
        copy.start()
        grad_out.append(copy)
    first_out.wait()
    for copy in grad_out:
        copy.wait()
    for copy in small + small_dots + pieces + over_pieces + over + [far_up, near_up] + up_own + up_next:
        copy.wait_send()
    for ring in rings[0] + rings[1] + rings[2] + sum_rings + [b_ring, n_ring, kv_ring, y_pieces, x_pieces]:
        ring.finish()
    for k in range(3):
        for i in range(2):
            for copy in across[k][i]:
                copy.wait_send()


def block(x, g, y, g2, docs, gain, w_query, w_key, w_value, w_out):
    return pl.pallas_call(
        block_kernel,
        name="block",
        out_shape=(
            jax.ShapeDtypeStruct((TOK, COLS), F32),
            jax.ShapeDtypeStruct((TOK, COLS), F32),
        ),
        in_specs=[ANY, ANY, ANY, ANY, VM, VM, ANY, ANY, ANY, ANY],
        out_specs=(ANY, ANY),
        scratch_shapes=[
            pltpu.VMEM((TOK, 128), F32),
            pltpu.VMEM((TOK, COLS), BF16),
            pltpu.VMEM((TOK, COLS), BF16),
            pltpu.VMEM((TOK, COLS), BF16),
            pltpu.VMEM((TOK, 1024), BF16),
            pltpu.VMEM((TOK, 1024), BF16),
            pltpu.VMEM((3, 4, 8, 32, 256), BF16),
            pltpu.VMEM((4, TOK, 256), BF16),
            pltpu.VMEM((4, TOK, COLS), BF16),
            pltpu.VMEM((4, TOK, COLS), BF16),
            pltpu.VMEM((WIDTH, 768), BF16),
            pltpu.VMEM((4, 512, COLS), BF16),
            pltpu.VMEM((TOK, 768), F32),
            pltpu.VMEM((TOK, 512), F32),
            pltpu.VMEM((TOK, COLS), BF16),
            pltpu.VMEM((2, 8, TOK), F32),
            pltpu.VMEM((2, 3, 8, TOK), F32),
            pltpu.VMEM((32, ROWS_KV, 256), BF16),
            pltpu.VMEM((BAND, TOK, 1024), F32),
            pltpu.VMEM((TOK, 256), BF16),
            pltpu.VMEM((256, 1024), BF16),
            pltpu.VMEM((1024, HEAD), BF16),
            pltpu.VMEM((HEAD, 1024), BF16),
            pltpu.VMEM((HEAD, 1024), F32),
            pltpu.VMEM((HEAD, 1024), F32),
            pltpu.VMEM((8, 1024), F32),
            pltpu.VMEM((8, 1024), F32),
            pltpu.VMEM((8, 1024), F32),
            pltpu.VMEM((8, 1024), F32),
            pltpu.VMEM((8, 1024), F32),
            pltpu.VMEM((TOK, 512), BF16),
            pltpu.VMEM((3, 4, 2, TOK, 256), BF16),
            pltpu.VMEM((3, 4, TOK, 256), BF16),
            pltpu.VMEM((3, 4, TOK, 256), BF16),
            pltpu.VMEM((3, 2, HALF, 256), BF16),
            pltpu.VMEM((3, 2, TOK, 256), BF16),
            pltpu.VMEM((2, TOK, 256), BF16),
            pltpu.VMEM((2, TOK, 256), BF16),
            pltpu.VMEM((2, HALF, COLS), BF16),
            pltpu.VMEM((2, TOK, COLS), BF16),
            pltpu.VMEM((2, HALF, COLS), BF16),
            pltpu.VMEM((2, TOK, COLS), BF16),
            pltpu.VMEM((TOK, 512), BF16),
            DMA((24,)),
            DMA((45,)),
            DMA((45,)),
            DMA((103,)),
            DMA((103,)),
        ],
        compiler_params=pltpu.CompilerParams(
            collective_id=0, has_side_effects=True, vmem_limit_bytes=63 * MIB
        ),
    )(x, g, y, g2, docs, gain, w_query, w_key, w_value, w_out)


def hand_on_kernel(a_ref, b_ref, a_out, b_out, a_buf, b_buf, sem):
    moves = []
    for n, (src, buf, dst) in enumerate(((a_ref, a_buf, a_out), (b_ref, b_buf, b_out))):
        for i in range(2):
            part = pl.ds(i * HALF, HALF)
            take = pltpu.make_async_copy(src.at[part], buf.at[part], sem.at[0, n, i])
            give = pltpu.make_async_copy(buf.at[part], dst.at[part], sem.at[1, n, i])
            take.start()
            moves.append((take, give))
    for take, give in moves:
        take.wait()
        give.start()
    for take, give in moves:
        give.wait()


def hand_on(a, b):
    shape = jax.ShapeDtypeStruct((TOK, COLS), F32)
    return pl.pallas_call(
        hand_on_kernel,
        name="hand_on",
        out_shape=(shape, shape),
        in_specs=[ANY, ANY],
        out_specs=(ANY, ANY),
        scratch_shapes=[
            pltpu.VMEM((TOK, COLS), F32),
            pltpu.VMEM((TOK, COLS), F32),
            DMA((2, 2, 2)),
        ],
        compiler_params=pltpu.CompilerParams(vmem_limit_bytes=63 * MIB),
    )(a, b)


def per_device(
    y_first, x_second, grad_first, grad_second, doc_ids, norm_gain, w_query, w_key, w_value, w_out
):
    first, grad = block(
        x_second, grad_first, y_first, grad_second, doc_ids.reshape(1, TOK), norm_gain.reshape(1, WIDTH),
        w_query, w_key, w_value, w_out,
    )
    return hand_on(first, grad)


def solution(mesh):
    placed = (
        P("seq", "mp"),
        P("seq", "mp"),
        P("seq", "mp"),
        P("seq", "mp"),
        P("seq"),
        P(),
        P(None, "mp"),
        P(None, "mp"),
        P(None, "mp"),
        P("mp", None),
    )
    return jax.shard_map(
        per_device,
        mesh=mesh,
        in_specs=placed,
        out_specs=(P("seq", "mp"), P("seq", "mp")),
        check_vma=False,
    )
```

time: 119 us -> 107 us (0.90)
  Pallas kernels: 112 us -> 106 us
  other arithmetic: 4.18 us -> 0 us
  local copies, waits for them, and re-layouts: 1.7 us -> 0 us
    pallas_call x1, Pallas kernels: 112 us -> 103 us  [block(): pl.pallas_call(block_kernel, name='block', out_shape=(jax.ShapeDtypeStruc...]
    add x1 -> x0, other arithmetic: 3.47 us -> none  [per_device(): x_grad = grad_second.astype(F32) + inverse * (shared * gain - unit * mean)]
    pallas_call x0 -> x1, Pallas kernels: none -> 2.42 us  [hand_on(): pl.pallas_call(hand_on_kernel, name='hand_on', out_shape=(shape, shape),...]
where the time goes in v3:
time: 107 us
  Pallas kernels  106 us (99%)
    pallas_call x1, Pallas kernels, block(): pl.pallas_call(block_kernel, name='block', out_shape=(jax.ShapeDtypeStruc...  103 us
    pallas_call x1, Pallas kernels, hand_on(): pl.pallas_call(hand_on_kernel, name='hand_on', out_shape=(shape, shape),...  2.42 us

profile of v3, /device:TPU:30, one launch (start us, length us, event | category | flops | bytes accessed | tf_op | source)
XLA Modules:
  0.0 106.7 jit_solution(16271875719946952726)
XLA Ops:
  0.6 103.4 %block.1 = (f32[256,1024]{1,0:T(8,128)}, f32[256,1024]{1,0:T(8,128)}) custom-call(bf16[256,1024]{1,0:T(8,128)(2,1)} %x_ref.1, bf16[256,1024]{1,0:T(8,128)(2,1)} %g_ref.1, bf16[256,1024]{1,0:T(8,128)(2,1)} %y_ref.1, bf16[256,1024]{1,0:T(8,128)(2,1)} %g2_ref.1, s32[1,256]{1,0:T(1,128)} %bitcast.3, f32[1,4096]{1,0:T(1,128)} %bitcast.2, ...), custom_call_target="tpu_custom_call" | custom-call | tf_op jit(solution)/shard_map/block/pallas_call | solution.py:692
  104.1 2.4 %hand_on.1 = (f32[256,1024]{1,0:T(8,128)}, f32[256,1024]{1,0:T(8,128)}) custom-call(f32[256,1024]{1,0:T(8,128)} %get-tuple-element.4.a_ref, f32[256,1024]{1,0:T(8,128)} %get-tuple-element.5.b_ref), custom_call_target="tpu_custom_call" | custom-call | tf_op jit(solution)/shard_map/hand_on/pallas_call | solution.py:775

commit v4 on v3

--- a/solution.py
+++ b/solution.py
@@ -568,16 +568,8 @@
     b_ring.forward()
     sweep(lambda b: back(b, 1), mid1, 8 * y)
     over[1].start()
-    x_pieces.wait_left()
-    x_pieces.wait_right()
-    x_pieces.wait_far()
-    for copy in over_pieces:
-        copy.start()
+    sweep(lambda b: back(b, 0), 8 * y, mid0)
     sum_rings[2].forward()
-    sweep(lambda b: back(b, 0), 8 * y, mid0)
-    open_ring(1)
-    yown[0] = sum_rings[2].wait_total()(whole).astype(BF16)
-    far_up.start()
     sweep(lambda b: back(b, 0), mid0, seq + 1)
     over[0].start()
     grads_q = dq_acc[...] * SCALE
@@ -599,11 +591,19 @@
     )
     norm_term(o)
     n_ring.start_far()
-    sum_rings[1].forward()
+    open_ring(1)
     norm_term(r)
     norm_term(l)
     n_ring.start_near()
+    yown[0] = sum_rings[2].wait_total()(whole).astype(BF16)
+    far_up.start()
     open_ring(0)
+    sum_rings[1].forward()
+    x_pieces.wait_left()
+    x_pieces.wait_right()
+    x_pieces.wait_far()
+    for copy in over_pieces:
+        copy.start()
     total = sum_rings[1].wait_total()(whole)
     far_up.wait_recv()
     yown[1] = (total + ynear[0].astype(F32)).astype(BF16)

time: 107 us -> 104 us (0.972); the launches traced: 107 us -> 102 us
  Pallas kernels: 106 us -> 102 us
    pallas_call x1, Pallas kernels: 103 us -> 99.2 us  [block(): pl.pallas_call(block_kernel, name='block', out_shape=(jax.ShapeDtypeStruc...]
where the time goes in v4:
time: 104 us; the launch traced here: 102 us
  Pallas kernels  102 us (98%)
    pallas_call x1, Pallas kernels, block(): pl.pallas_call(block_kernel, name='block', out_shape=(jax.ShapeDtypeStruc...  99.2 us
    pallas_call x1, Pallas kernels, hand_on(): pl.pallas_call(hand_on_kernel, name='hand_on', out_shape=(shape, shape),...  2.42 us

profile of v4, /device:TPU:30, one launch (start us, length us, event | category | flops | bytes accessed | tf_op | source)
XLA Modules:
  0.0 102.5 jit_solution(16248756835051752993)
XLA Ops:
  0.6 99.2 %block.1 = (f32[256,1024]{1,0:T(8,128)}, f32[256,1024]{1,0:T(8,128)}) custom-call(bf16[256,1024]{1,0:T(8,128)(2,1)} %x_ref.1, bf16[256,1024]{1,0:T(8,128)(2,1)} %g_ref.1, bf16[256,1024]{1,0:T(8,128)(2,1)} %y_ref.1, bf16[256,1024]{1,0:T(8,128)(2,1)} %g2_ref.1, s32[1,256]{1,0:T(1,128)} %bitcast.3, f32[1,4096]{1,0:T(1,128)} %bitcast.2, ...), custom_call_target="tpu_custom_call" | custom-call | tf_op jit(solution)/shard_map/block/pallas_call | solution.py:692
  99.9 2.4 %hand_on.1 = (f32[256,1024]{1,0:T(8,128)}, f32[256,1024]{1,0:T(8,128)}) custom-call(f32[256,1024]{1,0:T(8,128)} %get-tuple-element.4.a_ref, f32[256,1024]{1,0:T(8,128)} %get-tuple-element.5.b_ref), custom_call_target="tpu_custom_call" | custom-call | tf_op jit(solution)/shard_map/hand_on/pallas_call | solution.py:775
